TPU v7x, 128 devices: a whole 4x4x4 slice. The times are simulated.
128 devices in a mesh: ca: 8 (over y, core), fe: 16 (over z, x).
Axes of the slice: x: 4, y: 4, z: 4, core: 2. Of those that a mesh axis runs over, the one named last changes fastest.
Arguments:
- grain_ids: int32 [216, 262144], P(None, ('ca', 'fe')), may hold values from 0 to 4095
- euler_angles: float32 [3, 4096], replicated, may hold values from -3.140625 to 3.140625
- brick_active: int32 [262144], P(('ca', 'fe')), may hold values 0 or 1
- brick_owner: int32 [262144, 1], P(('ca', 'fe')), may hold values from 0 to 127, as said below
- brick_element: int32 [262144], P(('ca', 'fe')), may hold values from 0 to 224, as said below
- displacement: float32 [3, 128, 256], P(None, ('ca', 'fe')), may hold values from -0.3 to 0.3
- stress_old: float32 [6, 8, 28800], P(None, None, ('ca', 'fe')), may hold values from -3 to 3
- resistance: float32 [12, 8, 28800], P(None, None, ('ca', 'fe')), may hold values from 0.2 to 0.8
- quad_weights: int32 [8, 28800], P(None, ('ca', 'fe')), may hold values from 32768 to 98304
Outputs:
- stress_new: float32 [6, 8, 28800], P(None, None, ('ca', 'fe'))
- forces: float32 [3, 128, 256], P(None, ('ca', 'fe'))
Inputs may be any that keep to these rules, and one draw needn't show every extreme that they name: `brick_owner`: the bricks of one device name each owner at least 2048 / 256 times and at most 40 times; one owner is named exactly 40 times by the bricks of every device. `brick_element`: every element of every owner is named by at least one brick.
All inputs are finite; a program needn't handle non-finite values. No bound on the sum of `brick_active` on one device may be relied on, other than what follows from the above.
Results may differ from a plain program's by a relative error of at most 0.0002.
Values sent between devices are 32-bit elements; how exact they have to be, the bound alone decides.
A program may use at most 448 MiB of HBM per device.

v0:
```python
import math

import jax
import jax.numpy as jnp
from jax import lax
from jax.sharding import PartitionSpec as P

GX = 15


SLIP_PLANES = [
    [value / math.sqrt(3.0) for value in row]
    for row in [[1, 1, 1]] * 3 + [[-1, 1, 1]] * 3 + [[1, -1, 1]] * 3 + [[1, 1, -1]] * 3
]
SLIP_DIRECTIONS = [
    [value / math.sqrt(2.0) for value in row]
    for row in [
        [0, 1, -1],
        [1, 0, -1],
        [1, -1, 0],
        [0, 1, -1],
        [1, 0, 1],
        [1, 1, 0],
        [0, 1, 1],
        [1, 0, -1],
        [1, 1, 0],
        [0, 1, 1],
        [1, 0, 1],
        [1, -1, 0],
    ]
]
LAMBDA_ELASTIC = 1.5
SHEAR_MODULUS = 1.0
RATE_STEP = 0.1
FIXED_POINT = 65536.0


def passed_along(block, axis, distance):
    devices = range(lax.axis_size(axis))
    route = [(i - distance, i) for i in devices if i - distance in devices]
    return lax.ppermute(block, axis, route)


def shape_gradients():
    grad_table = [[[0.0, 0.0, 0.0] for corner in range(8)] for quadrature in range(8)]
    point_offset = 1.0 / math.sqrt(3.0)
    for quadrature in range(8):
        natural = [
            (2 * (quadrature >> shift_bits & 1) - 1) * point_offset for shift_bits in (2, 1, 0)
        ]
        for corner in range(8):
            sign_list = [2 * (corner >> shift_bits & 1) - 1 for shift_bits in (2, 1, 0)]
            factors = [1.0 + sign_list[axis_id] * natural[axis_id] for axis_id in range(3)]
            for direction in range(3):
                others = 1.0
                for axis_id in range(3):
                    if axis_id != direction:
                        others = others * factors[axis_id]
                grad_table[quadrature][corner][direction] = (
                    2.0 * sign_list[direction] * others / 8.0
                )
    return grad_table


def rotation_table(euler_angles):
    cos_one, sin_one = (jnp.cos(euler_angles[0]), jnp.sin(euler_angles[0]))
    cos_mid, sin_mid = (jnp.cos(euler_angles[1]), jnp.sin(euler_angles[1]))
    cos_two, sin_two = (jnp.cos(euler_angles[2]), jnp.sin(euler_angles[2]))
    entries_list = [
        cos_one * cos_two - sin_one * sin_two * cos_mid,
        -cos_one * sin_two - sin_one * cos_two * cos_mid,
        sin_one * sin_mid,
        sin_one * cos_two + cos_one * sin_two * cos_mid,
        -sin_one * sin_two + cos_one * cos_two * cos_mid,
        -cos_one * sin_mid,
        sin_two * sin_mid,
        cos_two * sin_mid,
        cos_mid,
    ]
    return jnp.stack(entries_list)


def octant_sums(rotation, grain_ids):
    per_octant = grain_ids.shape[0] // 8
    pieces = []
    for octant in range(8):
        picked = jnp.take(
            rotation, grain_ids[octant * per_octant : (octant + 1) * per_octant], axis=1
        )
        pieces.append(jnp.sum(picked, axis=1))
    return jnp.concatenate(pieces, axis=0)


def corner_values(padded, layers):
    corners = []
    for corner in range(8):
        step_x, step_y, step_z = (corner >> 2 & 1, corner >> 1 & 1, corner & 1)
        block_values = padded[
            :, :, step_z : step_z + layers, step_y : step_y + GX, step_x : step_x + GX
        ]
        corners.append(block_values.reshape(3, -1))
    return jnp.stack(corners, axis=1)


def element_update(padded, layers, orient, stress_old, resistance, quad_weights):
    grad_table = jnp.asarray(shape_gradients(), dtype=jnp.float32)
    corners = corner_values(padded, layers)
    gradients = jnp.einsum("cne,qnd->cdqe", corners, grad_table, precision=lax.Precision.HIGHEST)
    strain = [
        gradients[0, 0],
        gradients[1, 1],
        gradients[2, 2],
        0.5 * (gradients[1, 2] + gradients[2, 1]),
        0.5 * (gradients[0, 2] + gradients[2, 0]),
        0.5 * (gradients[0, 1] + gradients[1, 0]),
    ]
    volume = strain[0] + strain[1] + strain[2]
    trial_stress = []
    for component in range(6):
        change = 2.0 * SHEAR_MODULUS * strain[component]
        if component < 3:
            change = change + LAMBDA_ELASTIC * volume
        trial_stress.append(stress_old[component] + change)
    frames = orient.reshape(8, 3, 3, -1)
    correction = [jnp.zeros_like(trial_stress[0]) for component in range(6)]
    for system in range(12):
        rotated_dir = [
            frames[:, row_index, 0] * float(SLIP_DIRECTIONS[system][0])
            + frames[:, row_index, 1] * float(SLIP_DIRECTIONS[system][1])
            + frames[:, row_index, 2] * float(SLIP_DIRECTIONS[system][2])
            for row_index in range(3)
        ]
        rotated_normal = [
            frames[:, row_index, 0] * float(SLIP_PLANES[system][0])
            + frames[:, row_index, 1] * float(SLIP_PLANES[system][1])
            + frames[:, row_index, 2] * float(SLIP_PLANES[system][2])
            for row_index in range(3)
        ]
        schmid = [
            rotated_dir[0] * rotated_normal[0],
            rotated_dir[1] * rotated_normal[1],
            rotated_dir[2] * rotated_normal[2],
            0.5 * (rotated_dir[1] * rotated_normal[2] + rotated_dir[2] * rotated_normal[1]),
            0.5 * (rotated_dir[0] * rotated_normal[2] + rotated_dir[2] * rotated_normal[0]),
            0.5 * (rotated_dir[0] * rotated_normal[1] + rotated_dir[1] * rotated_normal[0]),
        ]
        resolved = (
            trial_stress[0] * schmid[0]
            + trial_stress[1] * schmid[1]
            + trial_stress[2] * schmid[2]
            + 2.0
            * (
                trial_stress[3] * schmid[3]
                + trial_stress[4] * schmid[4]
                + trial_stress[5] * schmid[5]
            )
        )
        slip_ratio = resolved / resistance[system]
        slip_step = RATE_STEP * slip_ratio * jnp.abs(slip_ratio)
        correction = [
            correction[component] + slip_step * schmid[component] for component in range(6)
        ]
    updated = [
        trial_stress[component] - 2.0 * SHEAR_MODULUS * correction[component]
        for component in range(6)
    ]
    stress_new = jnp.stack(updated)
    tensor = jnp.stack(
        [
            jnp.stack([updated[0], updated[5], updated[4]]),
            jnp.stack([updated[5], updated[1], updated[3]]),
            jnp.stack([updated[4], updated[3], updated[2]]),
        ]
    )
    point_scale = quad_weights.astype(jnp.float32) * (1.0 / (FIXED_POINT * 8.0))
    element_forces = jnp.einsum(
        "cdqe,qnd->cne", tensor * point_scale, grad_table, precision=lax.Precision.HIGHEST
    )
    component_count = padded.shape[1]
    nodal = jnp.zeros((3, component_count, layers + 1, GX + 1, GX + 1), jnp.float32)
    for corner in range(8):
        step_x, step_y, step_z = (corner >> 2 & 1, corner >> 1 & 1, corner & 1)
        nodal = nodal.at[
            :, :, step_z : step_z + layers, step_y : step_y + GX, step_x : step_x + GX
        ].add(element_forces[:, corner].reshape(3, component_count, layers, GX, GX))
    return (stress_new, nodal)


def body(
    grain_ids,
    euler_angles,
    brick_active,
    brick_owner,
    brick_element,
    displacement,
    stress_old,
    resistance,
    quad_weights,
):
    groups = lax.axis_size("ca")
    members = lax.axis_size("fe")
    devices = groups * members
    bricks = grain_ids.shape[1]
    capacity = 5 * bricks // (2 * devices)
    elements = stress_old.shape[2]
    layers = displacement.shape[1]
    rotation = rotation_table(euler_angles)
    active = brick_active.astype(jnp.float32)
    octant_total = octant_sums(rotation, grain_ids) * active[None]
    owner = brick_owner[:, 0]
    onehot = (owner[:, None] == jnp.arange(devices, dtype=jnp.int32)[None]).astype(jnp.int32)
    earlier = jnp.sum(jnp.cumsum(onehot, axis=0) * onehot, axis=1) - 1
    position = owner * capacity + earlier
    send_values = jnp.zeros((72, devices * capacity), jnp.float32).at[:, position].set(octant_total)
    label_values = jnp.where(brick_active > 0, brick_element, -1).astype(jnp.float32)
    send_labels = (
        jnp.full((1, devices * capacity), -1.0, jnp.float32).at[:, position].set(label_values[None])
    )
    got_values, got_labels = (
        lax.all_to_all(
            send_values.reshape(72, devices, capacity),
            ("ca", "fe"),
            split_axis=1,
            concat_axis=1,
            tiled=True,
        ),
        lax.all_to_all(
            send_labels.reshape(1, devices, capacity),
            ("ca", "fe"),
            split_axis=1,
            concat_axis=1,
            tiled=True,
        ),
    )
    values = got_values.reshape(72, devices * capacity)
    labels = got_labels.reshape(devices * capacity).astype(jnp.int32)
    slot_index = jnp.where(labels >= 0, labels, elements)
    gathered = (
        jnp.zeros((72, elements + 1), jnp.float32).at[:, slot_index].add(values)[:, :elements]
    )
    counts = (
        jnp.zeros((elements + 1,), jnp.float32)
        .at[slot_index]
        .add((labels >= 0).astype(jnp.float32))[:elements]
    )
    orient = gathered / (8.0 * jnp.maximum(counts, 1.0))
    upper_layer = passed_along(displacement, "fe", -1)
    node_field = jnp.concatenate([displacement, upper_layer], axis=1).reshape(
        3, 1, layers + 1, GX + 1, GX + 1
    )
    stress_new, nodal = element_update(
        node_field, layers, orient, stress_old, resistance, quad_weights
    )
    nodal = nodal.reshape(3, layers + 1, (GX + 1) * (GX + 1))
    owned_forces = nodal[:, :layers]
    top_partial = nodal[:, layers:]
    from_below = passed_along(top_partial, "fe", 1)
    forces = owned_forces.at[:, :1].add(from_below)
    return (stress_new, forces)


def solution(mesh):
    placed = (
        P(None, ("ca", "fe")),
        P(),
        P(("ca", "fe")),
        P(("ca", "fe"), None),
        P(("ca", "fe")),
        P(None, ("ca", "fe"), None),
        P(None, None, ("ca", "fe")),
        P(None, None, ("ca", "fe")),
        P(None, ("ca", "fe")),
    )
    return jax.shard_map(
        body,
        mesh=mesh,
        in_specs=placed,
        out_specs=(P(None, None, ("ca", "fe")), P(None, ("ca", "fe"), None)),
        check_vma=False,
    )
```

profile of v0, /device:TPU:1, one launch (start us, length us, event | category | flops | bytes accessed | tf_op | source)
XLA Modules:
  0.0 1698.0 jit_solution(15722385053783475020)
XLA Ops:
  5.1 8.1 scatter_custom_fusion
  13.9 12.0 all-to-all-start
  27.3 2.4 slice_cosine_fusion
  29.7 2.3 multiply_add_fusion.1
  32.0 2.9 compare_select_fusion
  34.9 3.1 compare_and_fusion
  40.9 182.1 %gather_fusion.6 = f32[55296,9]{1,0:T(8,128)} fusion(f32[9,4096]{0,1:T(8,128)S(1)} %copy.119, s32[55296]{0:T(1024)S(1)} %broadcast_clamp_fusion.1), kind=kCustom, calls=%fused_computation.6.clone | custom fusion | bytes 4202496 | tf_op jit(solution)/shard_map/jit(_take)/gather | solution.py:87
  223.0 182.0 %gather_fusion.7 = f32[55296,9]{1,0:T(8,128)} fusion(f32[9,4096]{0,1:T(8,128)S(1)} %copy.119, s32[55296]{0:T(1024)S(1)} %broadcast_clamp_fusion), kind=kCustom, calls=%fused_computation.7.clone | custom fusion | bytes 4202496 | tf_op jit(solution)/shard_map/jit(_take)/gather | solution.py:87
  406.0 182.0 %gather_fusion.4 = f32[55296,9]{1,0:T(8,128)} fusion(f32[9,4096]{0,1:T(8,128)S(1)} %copy.119, s32[55296]{0:T(1024)S(1)} %broadcast_clamp_fusion.3), kind=kCustom, calls=%fused_computation.4.clone | custom fusion | bytes 4202496 | tf_op jit(solution)/shard_map/jit(_take)/gather | solution.py:87
  589.1 182.0 %gather_fusion.5 = f32[55296,9]{1,0:T(8,128)} fusion(f32[9,4096]{0,1:T(8,128)S(1)} %copy.119, s32[55296]{0:T(1024)S(1)} %broadcast_clamp_fusion.2), kind=kCustom, calls=%fused_computation.5.clone | custom fusion | bytes 4202496 | tf_op jit(solution)/shard_map/jit(_take)/gather | solution.py:87
  772.1 182.0 %gather_fusion.2 = f32[55296,9]{1,0:T(8,128)} fusion(f32[9,4096]{0,1:T(8,128)S(1)} %copy.119, s32[55296]{0:T(1024)S(1)} %broadcast_clamp_fusion.5), kind=kCustom, calls=%fused_computation.2.clone | custom fusion | bytes 4202496 | tf_op jit(solution)/shard_map/jit(_take)/gather | solution.py:87
  954.2 182.1 %gather_fusion.3 = f32[55296,9]{1,0:T(8,128)} fusion(f32[9,4096]{0,1:T(8,128)S(1)} %copy.119, s32[55296]{0:T(1024)S(1)} %broadcast_clamp_fusion.4), kind=kCustom, calls=%fused_computation.3.clone | custom fusion | bytes 4202496 | tf_op jit(solution)/shard_map/jit(_take)/gather | solution.py:87
  1136.4 182.1 %gather_fusion = f32[55296,9]{1,0:T(8,128)} fusion(f32[9,4096]{0,1:T(8,128)S(1)} %copy.119, s32[55296]{0:T(1024)S(1)} %broadcast_clamp_fusion.7), kind=kCustom, calls=%fused_computation.clone | custom fusion | bytes 4202496 | tf_op jit(solution)/shard_map/jit(_take)/gather | solution.py:87
  1318.5 182.0 %gather_fusion.1 = f32[55296,9]{1,0:T(8,128)} fusion(f32[9,4096]{0,1:T(8,128)S(1)} %copy.119, s32[55296]{0:T(1024)S(1)} %broadcast_clamp_fusion.6), kind=kCustom, calls=%fused_computation.1.clone | custom fusion | bytes 4202496 | tf_op jit(solution)/shard_map/jit(_take)/gather | solution.py:87
  1500.6 21.0 %bitcast_reduce_fusion = (f32[9,2048]{0,1:T(8,128)S(1)}, f32[9,2048]{0,1:T(8,128)S(1)}) fusion(f32[27,2048,9]{2,1,0:T(8,128)} %bitcast.1208, pred[27,2048]{1,0:T(8,128)(4,1)S(1)} %copy-done.6, f32[27,2048,9]{2,1,0:T(8,128)} %bitcast.1207, pred[27,2048]{1,0:T(8,128)(4,1)S(1)} %copy-done.7), kind=kLoop, calls=%fused_computation.12 | loop fusion | flops 1953792 | bytes 4239360 | tf_op jit(solution)/shard_map/reduce_sum | solution.py:90
  1521.6 22.0 %bitcast_reduce_fusion.2 = (f32[9,2048]{0,1:T(8,128)S(1)}, f32[9,2048]{0,1:T(8,128)}) fusion(f32[27,2048,9]{2,1,0:T(8,128)} %bitcast.1210, pred[27,2048]{1,0:T(8,128)(4,1)S(1)} %copy-done.4, f32[27,2048,9]{2,1,0:T(8,128)} %bitcast.1209, pred[27,2048]{1,0:T(8,128)(4,1)S(1)} %copy-done.5), kind=kLoop, calls=%fused_computation.14 | loop fusion | flops 1953792 | bytes 4239360 | tf_op jit(solution)/shard_map/reduce_sum | solution.py:90
  1543.6 22.3 %bitcast_reduce_fusion.4 = (f32[9,2048]{0,1:T(8,128)}, f32[9,2048]{0,1:T(8,128)}) fusion(f32[27,2048,9]{2,1,0:T(8,128)} %bitcast.1213, pred[27,2048]{1,0:T(8,128)(4,1)S(1)} %copy-done.2, f32[27,2048,9]{2,1,0:T(8,128)} %bitcast.1211, pred[27,2048]{1,0:T(8,128)(4,1)S(1)} %copy-done.3), kind=kLoop, calls=%fused_computation.16 | loop fusion | flops 1953792 | bytes 4239360 | tf_op jit(solution)/shard_map/reduce_sum | solution.py:90
  1566.0 22.2 %bitcast_reduce_fusion.6 = (f32[9,2048]{0,1:T(8,128)}, f32[9,2048]{0,1:T(8,128)}) fusion(f32[27,2048,9]{2,1,0:T(8,128)} %bitcast.1214, pred[27,2048]{1,0:T(8,128)(4,1)S(1)} %copy-done, f32[27,2048,9]{2,1,0:T(8,128)} %bitcast.1212, pred[27,2048]{1,0:T(8,128)(4,1)S(1)} %copy-done.1), kind=kLoop, calls=%fused_computation.18 | loop fusion | flops 1953792 | bytes 4239360 | tf_op jit(solution)/shard_map/reduce_sum | solution.py:90
  1588.2 6.1 concatenate.37
  1594.3 8.7 scatter_custom_fusion.1
  1604.9 11.3 all-to-all-start.1
  1618.6 35.8 %scatter_custom_fusion.3 = f32[226]{0:T(256)S(1)} fusion(s32[5120]{0:T(1024)S(1)} %bitcast.1220, f32[5120]{0:T(1024)S(1)} %reshape.4087, f32[]{:T(128)} %constant.341.clone.1), kind=kCustom, calls=%fused_computation.532 | custom fusion | flops 5120 | bytes 908 | tf_op jit(solution)/shard_map/scatter-add | solution.py:244
  1654.4 29.7 %scatter_custom_fusion.2 = f32[72,226]{0,1:T(8,128)S(1)} fusion(s32[5120]{0:T(1024)S(1)} %bitcast.1221, f32[5120,72]{1,0:T(8,128)S(1)} %bitcast.1215, f32[]{:T(128)} %constant.341.clone.1), kind=kCustom, calls=%fused_computation.69 | custom fusion | flops 368640 | bytes 65092 | tf_op jit(solution)/shard_map/scatter-add | solution.py:239
  1693.3 3.3 collective-permute-start.1
  (125 shorter events, 27.2 us)
Async XLA Ops:
  4.3 33.7 %copy-start.11 = (s32[2048,1]{0,1:T(1,128)}, s32[2048,1]{0,1:T(1,128)S(1)}, u32[]{:S(2)}) copy-start(s32[2048,1]{0,1:T(1,128)S(1)} %compare_select_fusion.10) | copy-start | bytes 24580
  13.9 1591.0 %all-to-all-start = ((f32[1,128,40]{2,0,1:T(1,128)}), f32[1,128,40]{2,0,1:T(1,128)}, u32[]{:S(2)}, u32[]{:S(2)}) async-start(f32[1,128,40]{2,0,1:T(1,128)} %bitcast.12), calls=%async_computation | async-start | bytes 131072 | tf_op jit(solution)/shard_map/all_to_all | solution.py:227
  25.8 1577.1 %collective-permute-start = (f32[3,1,256]{2,1,0:T(1,128)}, f32[3,1,256]{2,1,0:T(1,128)}, u32[]{:S(2)}, u32[]{:S(2)}) collective-permute-start(f32[3,1,256]{2,1,0:T(1,128)} %param.37), channel_id=1, source_target_pairs={{1,0},{2,1},{3,2},{4,3},{5,4},{6,5},{7,6},{8,7},{9,8},{10,9},{11,1... | collective-permute-start | bytes 9224 | tf_op jit(solution)/shard_map/ppermute | solution.py:41
  954.2 546.4 %copy-start.6 = (pred[27,2048]{1,0:T(8,128)(4,1)S(1)}, pred[27,2048]{1,0:T(8,128)(4,1)}, u32[]{:S(2)}) copy-start(pred[27,2048]{1,0:T(8,128)(4,1)} %get-tuple-element.188) | copy-start | bytes 165892
  954.2 546.4 %copy-start.7 = (pred[27,2048]{1,0:T(8,128)(4,1)S(1)}, pred[27,2048]{1,0:T(8,128)(4,1)}, u32[]{:S(2)}) copy-start(pred[27,2048]{1,0:T(8,128)(4,1)} %get-tuple-element.189) | copy-start | bytes 165892
  1500.6 21.0 %copy-start.4 = (pred[27,2048]{1,0:T(8,128)(4,1)S(1)}, pred[27,2048]{1,0:T(8,128)(4,1)}, u32[]{:S(2)}) copy-start(pred[27,2048]{1,0:T(8,128)(4,1)} %get-tuple-element.190) | copy-start | bytes 165892
  1500.6 21.0 %copy-start.5 = (pred[27,2048]{1,0:T(8,128)(4,1)S(1)}, pred[27,2048]{1,0:T(8,128)(4,1)}, u32[]{:S(2)}) copy-start(pred[27,2048]{1,0:T(8,128)(4,1)} %get-tuple-element.191) | copy-start | bytes 165892
  1521.6 22.0 %copy-start.2 = (pred[27,2048]{1,0:T(8,128)(4,1)S(1)}, pred[27,2048]{1,0:T(8,128)(4,1)}, u32[]{:S(2)}) copy-start(pred[27,2048]{1,0:T(8,128)(4,1)} %get-tuple-element.192) | copy-start | bytes 165892
  1521.6 22.0 %copy-start.3 = (pred[27,2048]{1,0:T(8,128)(4,1)S(1)}, pred[27,2048]{1,0:T(8,128)(4,1)}, u32[]{:S(2)}) copy-start(pred[27,2048]{1,0:T(8,128)(4,1)} %get-tuple-element.193) | copy-start | bytes 165892
  1543.6 22.3 %copy-start = (pred[27,2048]{1,0:T(8,128)(4,1)S(1)}, pred[27,2048]{1,0:T(8,128)(4,1)}, u32[]{:S(2)}) copy-start(pred[27,2048]{1,0:T(8,128)(4,1)} %get-tuple-element.194) | copy-start | bytes 165892
  1543.6 22.3 %copy-start.1 = (pred[27,2048]{1,0:T(8,128)(4,1)S(1)}, pred[27,2048]{1,0:T(8,128)(4,1)}, u32[]{:S(2)}) copy-start(pred[27,2048]{1,0:T(8,128)(4,1)} %get-tuple-element.195) | copy-start | bytes 165892
  1565.9 22.3 %copy-start.12 = (s32[8,225]{1,0:T(8,128)S(1)}, s32[8,225]{1,0:T(8,128)}, u32[]{:S(2)}) copy-start(s32[8,225]{1,0:T(8,128)} %param.40) | copy-start | bytes 21604
  1565.9 37.0 %copy-start.13 = (f32[3,1,256]{2,1,0:T(1,128)S(1)}, f32[3,1,256]{2,1,0:T(1,128)}, u32[]{:S(2)}) copy-start(f32[3,1,256]{2,1,0:T(1,128)} %param.37) | copy-start | bytes 9220
  1566.0 38.7 %copy-start.9 = (f32[8,8,3,1]{1,0,2,3:T(8,128)S(1)}, f32[8,8,3,1]{1,0,2,3:T(8,128)}, u32[]{:S(2)}) copy-start(f32[8,8,3,1]{1,0,2,3:T(8,128)} %constant.366) | copy-start | bytes 2308
  1566.0 38.9 %copy-start.10 = (f32[6,8,225]{2,1,0:T(8,128)S(1)}, f32[6,8,225]{2,1,0:T(8,128)}, u32[]{:S(2)}) copy-start(f32[6,8,225]{2,1,0:T(8,128)} %param.38) | copy-start | bytes 129604
  1566.0 118.4 %copy-start.8 = (f32[12,8,225]{2,1,0:T(8,128)S(1)}, f32[12,8,225]{2,1,0:T(8,128)}, u32[]{:S(2)}) copy-start(f32[12,8,225]{2,1,0:T(8,128)} %param.39) | copy-start | bytes 259204
  1604.9 49.5 %all-to-all-start.1 = ((f32[72,128,40]{0,2,1:T(8,128)}), f32[72,128,40]{0,2,1:T(8,128)S(1)}, u32[]{:S(2)}, u32[]{:S(2)}) async-start(f32[72,128,40]{0,2,1:T(8,128)} %bitcast.31), calls=%async_computation.1 | async-start | bytes 5242880 | tf_op jit(solution)/shard_map/all_to_all | solution.py:220
  1684.8 13.1 copy-start.14
  1693.3 4.1 collective-permute-start.1
where the time goes:
time: 1700 us
  local copies, waits for them, and re-layouts  1490 us (88%)
  other arithmetic  180 us (11%)
  starting transfers between devices  28.1 us (2%)
    gather x8, local copies, waits for them, and re-layouts, octant_sums(): jnp.take(rotation, grain_ids[octant * per_octant:(octant + 1) * per_octan...  1460 us
    reduce_sum x4, other arithmetic, octant_sums(): pieces.append(jnp.sum(picked, axis=1))  87.5 us
    scatter-add x1, other arithmetic, body(): counts = jnp.zeros((elements + 1,), jnp.float32).at[slot_index].add((labe...  35.8 us
  transfers between devices with their start and end apart: 4, of which 1 were waited for; matrix products, arithmetic and copies ran while one was open for 95% of the time, Pallas kernels for 0%

commit v1 on v0

v1 whole, which is shorter than its diff:
```python
import functools
import math

import jax
import jax.numpy as jnp
import numpy as np
from jax import lax
from jax.experimental import pallas as pl
from jax.experimental.pallas import tpu as pltpu
from jax.sharding import PartitionSpec as P

GX = 15
NODES = 256
CAP = 40
DEVICES = 128
ROWS = 24
FIXED_STEPS = float(2**20 - 1)

SLIP_PLANES = [
    [value / math.sqrt(3.0) for value in row]
    for row in [[1, 1, 1]] * 3 + [[-1, 1, 1]] * 3 + [[1, -1, 1]] * 3 + [[1, 1, -1]] * 3
]
SLIP_DIRECTIONS = [
    [value / math.sqrt(2.0) for value in row]
    for row in [
        [0, 1, -1],
        [1, 0, -1],
        [1, -1, 0],
        [0, 1, -1],
        [1, 0, 1],
        [1, 1, 0],
        [0, 1, 1],
        [1, 0, -1],
        [1, 1, 0],
        [0, 1, 1],
        [1, 0, 1],
        [1, -1, 0],
    ]
]
LAMBDA_ELASTIC = 1.5
SHEAR_MODULUS = 1.0
RATE_STEP = 0.1
FIXED_POINT = 65536.0
VMEM_LIMIT = 48 << 20


def shape_gradients():
    grad_table = np.zeros((8, 8, 3))
    point_offset = 1.0 / math.sqrt(3.0)
    for quadrature in range(8):
        natural = [
            (2 * (quadrature >> shift_bits & 1) - 1) * point_offset for shift_bits in (2, 1, 0)
        ]
        for corner in range(8):
            sign_list = [2 * (corner >> shift_bits & 1) - 1 for shift_bits in (2, 1, 0)]
            factors = [1.0 + sign_list[axis_id] * natural[axis_id] for axis_id in range(3)]
            for direction in range(3):
                others = 1.0
                for axis_id in range(3):
                    if axis_id != direction:
                        others = others * factors[axis_id]
                grad_table[quadrature, corner, direction] = (
                    2.0 * sign_list[direction] * others / 8.0
                )
    return grad_table


def gradient_matrices():
    table = shape_gradients()
    grads = np.zeros((72, 24), np.float32)
    forces = np.zeros((24, 72), np.float32)
    for comp in range(3):
        for direction in range(3):
            for q in range(8):
                for corner in range(8):
                    value = table[q, corner, direction]
                    grads[(comp * 3 + direction) * 8 + q, comp * 8 + corner] = value
                    forces[comp * 8 + corner, (comp * 3 + direction) * 8 + q] = value
    return grads, forces


def lane_pick(row, lanes):
    return jnp.take_along_axis(row, lanes, axis=1, mode="promise_in_bounds")


def merge_tree(stack, value, index, bits):
    level = 0
    while index & 1:
        value = jnp.where(bits[level], value, stack.pop())
        level += 1
        index >>= 1
    stack.append(value)


def build_table(euler_ref, table_ref):
    half_sum = 0.5 * (euler_ref[0] + euler_ref[2])
    half_diff = 0.5 * (euler_ref[0] - euler_ref[2])
    half_mid = 0.5 * euler_ref[1]
    cos_mid, sin_mid = jnp.cos(half_mid), jnp.sin(half_mid)
    real = cos_mid * jnp.cos(half_sum)
    flip = jnp.where(real < 0.0, -1.0, 1.0)
    scale = flip * FIXED_STEPS / (1.0 + jnp.abs(real))
    first = jnp.round(sin_mid * jnp.cos(half_diff) * scale).astype(jnp.int32)
    second = jnp.round(sin_mid * jnp.sin(half_diff) * scale).astype(jnp.int32)
    third = jnp.round(cos_mid * jnp.sin(half_sum) * scale).astype(jnp.int32)
    word_a = jnp.left_shift(first, 11) | (jnp.right_shift(third, 10) & 0x7FF)
    word_b = jnp.left_shift(second, 11) | (third & 0x3FF)
    for row in range(32):
        table_ref[row] = jnp.broadcast_to(word_a[row : row + 1], (8, 128))
        table_ref[32 + row] = jnp.broadcast_to(word_b[row : row + 1], (8, 128))


def lookup(table_ref, ids):
    lanes = ids & 127
    bits = [(ids & (128 << level)) != 0 for level in range(5)]
    words = ([], [])
    for row in range(32):
        for n, stack in enumerate(words):
            merge_tree(stack, lane_pick(table_ref[n * 32 + row], lanes), row, bits)
    return words[0][0], words[1][0]


def rotation_terms(word_a, word_b):
    a = jnp.right_shift(word_a, 11).astype(jnp.float32)
    b = jnp.right_shift(word_b, 11).astype(jnp.float32)
    c_bits = jnp.right_shift(jnp.left_shift(word_a, 21), 11) | (word_b & 0x3FF)
    c = c_bits.astype(jnp.float32)
    unit = 1.0 / FIXED_STEPS
    square = (a * a + b * b + c * c) * (unit * unit)
    inverse = 1.0 / (1.0 + square)
    inverse_square = inverse * inverse
    quad = inverse_square * (8.0 * unit * unit)
    lin = inverse_square * ((1.0 - square) * (4.0 * unit))
    qa, qb, qc = quad * a, quad * b, quad * c
    return [qa * a, qb * b, qc * c, qa * b, qa * c, qb * c, lin * a, lin * b, lin * c]


def sum_sublanes(parts, row):
    low4 = row < 4
    level = [
        jnp.where(low4, parts[q], parts[q + 4])
        + pltpu.roll(jnp.where(low4, parts[q + 4], parts[q]), 4, 0)
        for q in range(4)
    ]
    for step in (2, 1):
        keep = (row & step) == 0
        merged = []
        for q in range(step):
            other = jnp.where(keep, level[q + step], level[q])
            moved = jnp.where(keep, pltpu.roll(other, 8 - step, 0), pltpu.roll(other, step, 0))
            merged.append(jnp.where(keep, level[q], level[q + step]) + moved)
        level = merged
    return level[0]


def octant_kernel(ids_ref, euler_ref, out_ref, table_ref, part_ref):
    build_table(euler_ref, table_ref)
    row = lax.broadcasted_iota(jnp.int32, (8, 128), 0)
    tiles = ids_ref.shape[0] // 8
    per_octant = ids_ref.shape[0] // 8

    @pl.loop(0, ids_ref.shape[1] // 128)
    def _(block):
        columns = pl.ds(pl.multiple_of(block * 128, 128), 128)
        sums = None
        octant = 0
        for t in range(tiles):
            terms = rotation_terms(*lookup(table_ref, ids_ref[8 * t : 8 * t + 8, columns]))
            end = (octant + 1) * per_octant
            if 8 * t + 8 < end:
                sums = terms if sums is None else [s + v for s, v in zip(sums, terms)]
                continue
            split = end - 8 * t
            inside = row < split
            head = terms if split == 8 else [jnp.where(inside, v, 0.0) for v in terms]
            done = head if sums is None else [s + v for s, v in zip(sums, head)]
            for n in range(9):
                part_ref[n * 8 + octant] = done[n]
            sums = None if split == 8 else [jnp.where(inside, 0.0, v) for v in terms]
            octant += 1
        xx, yy, zz, xy, xz, yz, wx, wy, wz = [
            sum_sublanes([part_ref[n * 8 + q] for q in range(8)], row) for n in range(9)
        ]
        total = float(per_octant)
        entries = [
            total - (yy + zz),
            xy - wz,
            xz + wy,
            xy + wz,
            total - (xx + zz),
            yz - wx,
            xz - wy,
            yz + wx,
            total - (xx + yy),
        ]
        for n in range(9):
            out_ref[n, :, columns] = entries[n]


def octant_totals(grain_ids, euler_angles):
    bricks = grain_ids.shape[1]
    return pl.pallas_call(
        octant_kernel,
        out_shape=jax.ShapeDtypeStruct((9, 8, bricks), jnp.float32),
        in_specs=[pl.BlockSpec(memory_space=pltpu.VMEM)] * 2,
        out_specs=pl.BlockSpec(memory_space=pltpu.VMEM),
        scratch_shapes=[
            pltpu.VMEM((64, 8, 128), jnp.int32),
            pltpu.VMEM((72, 8, 128), jnp.float32),
        ],
        compiler_params=pltpu.CompilerParams(vmem_limit_bytes=VMEM_LIMIT),
        name="octant_totals",
    )(grain_ids, euler_angles.reshape(3, 32, 128))


NT_DIMS = (((1,), (1,)), ((), ()))


def slot_kernel(total_ref, owner_ref, element_ref, active_ref, out_ref, pick_ref, slot_ref):
    span = 256
    device = lax.broadcasted_iota(jnp.int32, (DEVICES, span), 0)
    slot = lax.broadcasted_iota(jnp.int32, (CAP, span), 0)
    brick = lax.broadcasted_iota(jnp.int32, (1, span), 1)
    before = (
        lax.broadcasted_iota(jnp.int32, (span, span), 0)
        < lax.broadcasted_iota(jnp.int32, (span, span), 1)
    ).astype(jnp.bfloat16)
    ones = jnp.ones((span, span), jnp.bfloat16)
    carry = jnp.zeros((DEVICES, span), jnp.float32)
    found = jnp.zeros((3 * CAP, DEVICES), jnp.float32)
    for start in range(0, total_ref.shape[2], span):
        owned = device == owner_ref[:, start : start + span]
        owned_half = owned.astype(jnp.bfloat16)
        earlier = carry + jnp.dot(owned_half, before, preferred_element_type=jnp.float32)
        carry = carry + jnp.dot(owned_half, ones, preferred_element_type=jnp.float32)
        rank = jnp.sum(jnp.where(owned, earlier, 0.0), axis=0, keepdims=True)
        mine = slot == rank.astype(jnp.int32)
        label = jnp.where(
            active_ref[:, start : start + span] > 0, element_ref[:, start : start + span] + 1, 0
        )
        values = [(brick + start) >> 7, (brick + start) & 127, label]
        left = jnp.concatenate(
            [jnp.where(mine, value.astype(jnp.float32), 0.0) for value in values], axis=0
        ).astype(jnp.bfloat16)
        found = found + lax.dot_general(
            left, owned_half, NT_DIMS, preferred_element_type=jnp.float32
        )
    pick_ref[...] = found[: 2 * CAP].astype(jnp.int32)
    words = 72 * CAP
    slot_ref[words : words + CAP] = found[2 * CAP :]
    slot_ref[words + CAP :] = jnp.zeros((slot_ref.shape[0] - words - CAP, 128), jnp.float32)
    blocks = total_ref.shape[2] // 128
    depth = blocks.bit_length() - 1
    tiles = CAP // 8

    @pl.loop(0, 9)
    def _(entry):
        for t in range(tiles):
            lanes = pick_ref[CAP + 8 * t : CAP + 8 * t + 8]
            high = pick_ref[8 * t : 8 * t + 8]
            bits = [(high & (1 << level)) != 0 for level in range(depth)]
            for q in range(8):
                stack = []
                for block in range(blocks):
                    values = jnp.broadcast_to(
                        total_ref[entry, q : q + 1, block * 128 : block * 128 + 128], (8, 128)
                    )
                    merge_tree(stack, lane_pick(values, lanes), block, bits)
                row = pl.multiple_of((entry * 8 + q) * CAP + 8 * t, 8)
                slot_ref[pl.ds(row, 8), :] = stack[0]

    for c in range(ROWS):
        if c < slot_ref.shape[0] // 128:
            flipped = slot_ref[c * 128 : c * 128 + 128].T
        else:
            flipped = jnp.zeros((128, 128), jnp.float32)
        out_ref[pl.ds(c, DEVICES, stride=ROWS), :] = flipped


def slots_to_send(totals, owner, element, active):
    bricks = totals.shape[2]
    return pl.pallas_call(
        slot_kernel,
        out_shape=jax.ShapeDtypeStruct((DEVICES * ROWS, 128), jnp.float32),
        in_specs=[pl.BlockSpec(memory_space=pltpu.VMEM)] * 4,
        out_specs=pl.BlockSpec(memory_space=pltpu.VMEM),
        scratch_shapes=[
            pltpu.VMEM((2 * CAP, 128), jnp.int32),
            pltpu.VMEM(((ROWS - 1) * 128, 128), jnp.float32),
        ],
        compiler_params=pltpu.CompilerParams(vmem_limit_bytes=VMEM_LIMIT),
        name="slots_to_send",
    )(totals, owner.reshape(1, bricks), element.reshape(1, bricks), active.reshape(1, bricks))


def split_three(values):
    high = values.astype(jnp.bfloat16)
    rest = values - high.astype(jnp.float32)
    mid = rest.astype(jnp.bfloat16)
    low = (rest - mid.astype(jnp.float32)).astype(jnp.bfloat16)
    return jnp.concatenate([high, mid, low], axis=0)


def joined_three(product):
    rows = product.shape[0] // 3
    return product[:rows] + product[rows : 2 * rows] + product[2 * rows :]


def element_kernel(
    got_ref,
    below_ref,
    above_ref,
    stress_ref,
    resistance_ref,
    weights_ref,
    grads_ref,
    gather_ref,
    stress_out,
    owned_out,
    top_out,
    slot_ref,
):
    elements = stress_ref.shape[2]
    for c in range(ROWS - 1):
        slot_ref[c * 128 : c * 128 + 128] = got_ref[pl.ds(c, DEVICES, stride=ROWS), :].T
    sums = jnp.zeros((160, NODES), jnp.float32)
    label_value = lax.broadcasted_iota(jnp.int32, (NODES, 128), 0).astype(jnp.float32) + 1.0
    ones = jnp.ones((16, 128), jnp.bfloat16)
    for r in range(0, CAP, 2):
        left, right = [], []
        for n in (r, r + 1):
            values = slot_ref[pl.ds(n, 72, stride=CAP), :]
            high = values.astype(jnp.bfloat16).astype(jnp.float32)
            left.append(
                jnp.concatenate(
                    [jnp.concatenate([high, values - high], axis=0).astype(jnp.bfloat16), ones],
                    axis=0,
                )
            )
            hit = label_value == slot_ref[72 * CAP + n : 72 * CAP + n + 1]
            right.append(hit.astype(jnp.bfloat16))
        sums = sums + lax.dot_general(
            jnp.concatenate(left, axis=1),
            jnp.concatenate(right, axis=1),
            NT_DIMS,
            preferred_element_type=jnp.float32,
        )
    counts = sums[144:145]
    orient = (sums[:72] + sums[72:144]) / (8.0 * jnp.maximum(counts, 1.0))

    node = lax.broadcasted_iota(jnp.int32, (NODES, NODES), 0)
    lane = lax.broadcasted_iota(jnp.int32, (NODES, NODES), 1)
    base = lane
    for bound in range(GX, GX * GX, GX):
        base = base + jnp.where(lane >= bound, 1, 0)
    to_element = ((node == base) & (lane < elements)).astype(jnp.bfloat16)
    rows = []
    for comp in range(3):
        for corner in range(8):
            step_x, step_y, step_z = (corner >> 2 & 1, corner >> 1 & 1, corner & 1)
            source = above_ref if step_z else below_ref
            offset = step_y * (GX + 1) + step_x
            line = source[comp : comp + 1, :]
            rows.append(line if offset == 0 else pltpu.roll(line, NODES - offset, 1))
    corners = joined_three(
        jnp.dot(
            split_three(jnp.concatenate(rows, axis=0)),
            to_element,
            preferred_element_type=jnp.float32,
        )
    )
    gradients = jnp.dot(
        grads_ref[...],
        corners,
        precision=lax.Precision.HIGHEST,
        preferred_element_type=jnp.float32,
    )

    def grad(comp, direction):
        n = (comp * 3 + direction) * 8
        return gradients[n : n + 8, :elements]

    strain = [
        grad(0, 0),
        grad(1, 1),
        grad(2, 2),
        0.5 * (grad(1, 2) + grad(2, 1)),
        0.5 * (grad(0, 2) + grad(2, 0)),
        0.5 * (grad(0, 1) + grad(1, 0)),
    ]
    volume = strain[0] + strain[1] + strain[2]
    trial = []
    for component in range(6):
        change = 2.0 * SHEAR_MODULUS * strain[component]
        if component < 3:
            change = change + LAMBDA_ELASTIC * volume
        trial.append(stress_ref[component] + change)

    def frame(i, j):
        n = (i * 3 + j) * 8
        return orient[n : n + 8, :elements]

    def rotated(vector):
        out = []
        for i in range(3):
            terms = [float(vector[j]) * frame(i, j) for j in range(3) if vector[j] != 0.0]
            out.append(functools.reduce(lambda x, y: x + y, terms))
        return out

    normals = {tuple(vector): rotated(vector) for vector in SLIP_PLANES}
    correction = [jnp.zeros_like(trial[0]) for component in range(6)]
    for system in range(12):
        d = rotated(SLIP_DIRECTIONS[system])
        m = normals[tuple(SLIP_PLANES[system])]
        schmid = [
            d[0] * m[0],
            d[1] * m[1],
            d[2] * m[2],
            0.5 * (d[1] * m[2] + d[2] * m[1]),
            0.5 * (d[0] * m[2] + d[2] * m[0]),
            0.5 * (d[0] * m[1] + d[1] * m[0]),
        ]
        resolved = (
            trial[0] * schmid[0]
            + trial[1] * schmid[1]
            + trial[2] * schmid[2]
            + 2.0 * (trial[3] * schmid[3] + trial[4] * schmid[4] + trial[5] * schmid[5])
        )
        ratio = resolved / resistance_ref[system]
        slip_step = RATE_STEP * ratio * jnp.abs(ratio)
        correction = [
            correction[component] + slip_step * schmid[component] for component in range(6)
        ]
    updated = [
        trial[component] - 2.0 * SHEAR_MODULUS * correction[component] for component in range(6)
    ]
    for component in range(6):
        stress_out[component] = updated[component]
    scale = weights_ref[...].astype(jnp.float32) * (1.0 / (FIXED_POINT * 8.0))
    order = [0, 5, 4, 5, 1, 3, 4, 3, 2]
    pad = jnp.zeros((8, NODES - elements), jnp.float32)
    tensor = jnp.concatenate(
        [jnp.concatenate([updated[component] * scale, pad], axis=1) for component in order], axis=0
    )
    element_forces = jnp.dot(
        gather_ref[...],
        tensor,
        precision=lax.Precision.HIGHEST,
        preferred_element_type=jnp.float32,
    )
    placed = joined_three(
        lax.dot_general(
            split_three(element_forces), to_element, NT_DIMS, preferred_element_type=jnp.float32
        )
    )
    for out, step_z in ((owned_out, 0), (top_out, 1)):
        for comp in range(3):
            line = jnp.zeros((1, NODES), jnp.float32)
            for corner in range(8):
                if (corner & 1) != step_z:
                    continue
                offset = (corner >> 1 & 1) * (GX + 1) + (corner >> 2 & 1)
                part = placed[comp * 8 + corner : comp * 8 + corner + 1]
                line = line + (part if offset == 0 else pltpu.roll(part, offset, 1))
            out[comp : comp + 1, :] = line


def element_update(got, below, above, stress_old, resistance, quad_weights):
    grads, forces = gradient_matrices()
    layer = jax.ShapeDtypeStruct((3, NODES), jnp.float32)
    return pl.pallas_call(
        element_kernel,
        out_shape=(jax.ShapeDtypeStruct(stress_old.shape, jnp.float32), layer, layer),
        in_specs=[pl.BlockSpec(memory_space=pltpu.VMEM)] * 8,
        out_specs=(pl.BlockSpec(memory_space=pltpu.VMEM),) * 3,
        scratch_shapes=[pltpu.VMEM(((ROWS - 1) * 128, 128), jnp.float32)],
        compiler_params=pltpu.CompilerParams(vmem_limit_bytes=VMEM_LIMIT),
        name="element_update",
    )(
        got,
        below,
        above,
        stress_old,
        resistance,
        quad_weights,
        jnp.asarray(grads),
        jnp.asarray(forces),
    )


def passed_along(block, axis, distance):
    devices = range(lax.axis_size(axis))
    route = [(i - distance, i) for i in devices if i - distance in devices]
    return lax.ppermute(block, axis, route)


def body(
    grain_ids,
    euler_angles,
    brick_active,
    brick_owner,
    brick_element,
    displacement,
    stress_old,
    resistance,
    quad_weights,
):
    below = displacement[:, 0]
    above = passed_along(below, "fe", -1)
    totals = octant_totals(grain_ids, euler_angles)
    send = slots_to_send(totals, brick_owner, brick_element, brick_active)
    got = lax.all_to_all(
        send.reshape(DEVICES, ROWS, 128), ("ca", "fe"), split_axis=0, concat_axis=0, tiled=True
    )
    stress_new, owned, top = element_update(
        got.reshape(DEVICES * ROWS, 128), below, above, stress_old, resistance, quad_weights
    )
    forces = owned + passed_along(top, "fe", 1)
    return (stress_new, forces[:, None])


def solution(mesh):
    placed = (
        P(None, ("ca", "fe")),
        P(),
        P(("ca", "fe")),
        P(("ca", "fe"), None),
        P(("ca", "fe")),
        P(None, ("ca", "fe"), None),
        P(None, None, ("ca", "fe")),
        P(None, None, ("ca", "fe")),
        P(None, ("ca", "fe")),
    )
    return jax.shard_map(
        body,
        mesh=mesh,
        in_specs=placed,
        out_specs=(P(None, None, ("ca", "fe")), P(None, ("ca", "fe"), None)),
        check_vma=False,
    )
```

time: 1700 us -> 91.5 us (0.05)
  the two profiles are of different devices: /device:TPU:1 before, /device:TPU:32 now
where the time goes in v1:
time: 91.5 us; the launch traced here: 91.2 us
  Pallas kernels  45.5 us (50%)
  waiting for transfers between devices  24.6 us (27%)
  starting transfers between devices  17.4 us (19%)
  local copies, waits for them, and re-layouts  2.96 us (3%)
    pallas_call x1, Pallas kernels, octant_totals(): pl.pallas_call(octant_kernel, out_shape=jax.ShapeDtypeStruct((9, 8, brick...  33.7 us
    ppermute x2, waiting for transfers between devices, passed_along(): return lax.ppermute(block, axis, route)  19.1 us
    all_to_all x1, starting transfers between devices, body(): lax.all_to_all(send.reshape(DEVICES, ROWS, 128), ('ca', 'fe'), split_axis...  10.2 us
    pallas_call x1, Pallas kernels, slots_to_send(): pl.pallas_call(slot_kernel, out_shape=jax.ShapeDtypeStruct((DEVICES * ROW...  9.43 us
    ppermute x2, starting transfers between devices, passed_along(): return lax.ppermute(block, axis, route)  7.17 us
    all_to_all x1, waiting for transfers between devices, body(): lax.all_to_all(send.reshape(DEVICES, ROWS, 128), ('ca', 'fe'), split_axis...  5.43 us
    unnamed x23, local copies, waits for them, and re-layouts  2.96 us
    pallas_call x1, Pallas kernels, element_update(): pl.pallas_call(element_kernel, out_shape=(jax.ShapeDtypeStruct(stress_old...  2.38 us
  transfers between devices with their start and end apart: 3, of which 3 were waited for; matrix products, arithmetic and copies ran while one was open for 0% of the time, Pallas kernels for 0%

profile of v1, /device:TPU:32, one launch (start us, length us, event | category | flops | bytes accessed | tf_op | source)
XLA Modules:
  0.0 91.2 jit_solution(2318879738357875396)
XLA Ops:
  0.6 0.0 copy-start.5
  0.6 0.0 copy-start.6
  0.7 0.0 copy-start.7
  0.7 0.9 copy.18
  1.5 1.5 %copy-done = s32[216,2048]{1,0:T(8,128)S(1)} copy-done((s32[216,2048]{1,0:T(8,128)S(1)}, s32[216,2048]{1,0:T(8,128)}, u32[]{:S(2)}) %copy-start) | copy-done | bytes 1769496
  3.0 33.7 %octant_totals.1.total_ref = f32[9,8,2048]{2,1,0:T(8,128)S(1)} custom-call(s32[216,2048]{1,0:T(8,128)S(1)} %copy-done, f32[3,32,128]{2,1,0:T(8,128)S(1)} %bitcast.15), custom_call_target="tpu_custom_call" | custom-call | tf_op jit(solution)/shard_map/octant_totals/pallas_call | solution.py:202
  36.7 0.0 copy-done.5
  36.7 0.0 copy-done.6
  36.7 0.0 copy-done.7
  36.7 9.4 %slots_to_send.1 = f32[3072,128]{1,0:T(8,128)} custom-call(f32[9,8,2048]{2,1,0:T(8,128)S(1)} %octant_totals.1.total_ref, s32[1,2048]{1,0:T(1,128)S(1)} %bitcast.18, s32[1,2048]{1,0:T(1,128)S(1)} %bitcast.19, s32[1,2048]{1,0:T(1,128)S(1)} %bitcast.20), custom_call_target="tpu_custom_call" | custom-call | tf_op jit(solution)/shard_map/slots_to_send/pallas_call | solution.py:282
  46.2 0.0 copy-start.4
  46.2 0.0 copy-start.8
  46.2 10.2 %all-to-all-start = ((f32[128,24,128]{2,1,0:T(8,128)}), f32[128,24,128]{2,1,0:T(8,128)S(1)}, u32[]{:S(2)}, u32[]{:S(2)}) async-start(f32[128,24,128]{2,1,0:T(8,128)} %bitcast.3), calls=%async_computation | async-start | bytes 3145728 | tf_op jit(solution)/shard_map/all_to_all | solution.py:512
  56.4 0.0 copy-done.9
  56.5 4.5 %collective-permute-start = (f32[3,256]{1,0:T(4,128)S(1)}, f32[3,256]{1,0:T(4,128)S(1)}, u32[]{:S(2)}, u32[]{:S(2)}) collective-permute-start(f32[3,256]{1,0:T(4,128)S(1)} %bitcast.16), channel_id=1, source_target_pairs={{1,0},{2,1},{3,2},{4,3},{5,4},{6,5},{7,6},{8,7},{9,8},{10,9},{11,1... | collective-permute-start | bytes 9224 | tf_op jit(solution)/shard_map/ppermute | solution.py:494
  60.9 14.3 %collective-permute-done.above_ref = f32[3,256]{1,0:T(4,128)S(1)} collective-permute-done((f32[3,256]{1,0:T(4,128)S(1)}, f32[3,256]{1,0:T(4,128)S(1)}, u32[]{:S(2)}, u32[]{:S(2)}) %collective-permute-start) | collective-permute-done | bytes 3104 | tf_op jit(solution)/shard_map/ppermute | solution.py:494
  75.2 5.4 %all-to-all-done = f32[128,24,128]{2,1,0:T(8,128)S(1)} async-done(((f32[128,24,128]{2,1,0:T(8,128)}), f32[128,24,128]{2,1,0:T(8,128)S(1)}, u32[]{:S(2)}, u32[]{:S(2)}) %all-to-all-start) | async-done | bytes 1572896 | tf_op jit(solution)/shard_map/all_to_all | solution.py:512
  80.6 0.0 copy-done.1
  80.6 0.0 copy-done.2
  80.6 0.0 copy-done.3
  80.7 2.4 %element_update.1 = (f32[6,8,225]{2,1,0:T(8,128)}, f32[3,256]{1,0:T(4,128)S(1)}, f32[3,256]{1,0:T(4,128)S(1)}) custom-call(f32[3072,128]{1,0:T(8,128)S(1)} %bitcast.14, f32[3,256]{1,0:T(4,128)S(1)} %bitcast.17, f32[3,256]{1,0:T(4,128)S(1)} %collective-permute-done.above_ref, f32[6,8,225]{2,1,0:T(8,128)S(1)} %copy-done.2, f32[12,8,225]{2,1,0:T(8,128)S(1)} %copy-done.1, ...), custom_call_target="tpu_custom_call" | custom-call | tf_op jit(solution)/shard_map/element_update/pallas_call | solution.py:471
  83.0 2.7 %collective-permute-start.1 = (f32[3,256]{1,0:T(4,128)S(1)}, f32[3,256]{1,0:T(4,128)S(1)}, u32[]{:S(2)}, u32[]{:S(2)}) collective-permute-start(f32[3,256]{1,0:T(4,128)S(1)} %get-tuple-element.7), channel_id=1, source_target_pairs={{0,1},{1,2},{2,3},{3,4},{4,5},{5,6},{6,7},{7,8},{8,9},{9,10},{10,1... | collective-permute-start | bytes 9224 | tf_op jit(solution)/shard_map/ppermute | solution.py:494
  85.8 4.9 %collective-permute-done.1 = f32[3,256]{1,0:T(4,128)S(1)} collective-permute-done((f32[3,256]{1,0:T(4,128)S(1)}, f32[3,256]{1,0:T(4,128)S(1)}, u32[]{:S(2)}, u32[]{:S(2)}) %collective-permute-start.1) | collective-permute-done | bytes 3104 | tf_op jit(solution)/shard_map/ppermute | solution.py:494
  90.6 0.6 copy.13
  (9 shorter events, 0.0 us)
Async XLA Ops:
  0.6 36.1 %copy-start.5 = (s32[2048,1]{0,1:T(1,128)S(1)}, s32[2048,1]{0,1:T(1,128)}, u32[]{:S(2)}) copy-start(s32[2048,1]{0,1:T(1,128)} %param.14) | copy-start | bytes 24580
  0.6 36.1 %copy-start.6 = (s32[2048]{0:T(1024)S(1)}, s32[2048]{0:T(1024)}, u32[]{:S(2)}) copy-start(s32[2048]{0:T(1024)} %param.15) | copy-start | bytes 24580
  0.7 36.1 %copy-start.7 = (s32[2048]{0:T(1024)S(1)}, s32[2048]{0:T(1024)}, u32[]{:S(2)}) copy-start(s32[2048]{0:T(1024)} %param.13) | copy-start | bytes 24580
  1.5 1.5 %copy-start = (s32[216,2048]{1,0:T(8,128)S(1)}, s32[216,2048]{1,0:T(8,128)}, u32[]{:S(2)}) copy-start(s32[216,2048]{1,0:T(8,128)} %ids_ref.1) | copy-start | bytes 5308420
  46.2 10.3 %copy-start.9 = (f32[3,1,256]{2,1,0:T(1,128)S(1)}, f32[3,1,256]{2,1,0:T(1,128)}, u32[]{:S(2)}) copy-start(f32[3,1,256]{2,1,0:T(1,128)} %param.16) | copy-start | bytes 9220
  46.2 34.5 %copy-start.1 = (f32[12,8,225]{2,1,0:T(8,128)S(1)}, f32[12,8,225]{2,1,0:T(8,128)}, u32[]{:S(2)}) copy-start(f32[12,8,225]{2,1,0:T(8,128)} %resistance_ref.1) | copy-start | bytes 259204
  46.2 34.5 %copy-start.2 = (f32[6,8,225]{2,1,0:T(8,128)S(1)}, f32[6,8,225]{2,1,0:T(8,128)}, u32[]{:S(2)}) copy-start(f32[6,8,225]{2,1,0:T(8,128)} %stress_ref.1) | copy-start | bytes 129604
  46.2 34.5 %copy-start.3 = (f32[72,24]{1,0:T(8,128)S(1)}, f32[72,24]{1,0:T(8,128)}, u32[]{:S(2)}) copy-start(f32[72,24]{1,0:T(8,128)} %constant.4.clone.grads_ref) | copy-start | bytes 20740
  46.2 34.5 %copy-start.4 = (f32[24,72]{1,0:T(8,128)S(1)}, f32[24,72]{1,0:T(8,128)}, u32[]{:S(2)}) copy-start(f32[24,72]{1,0:T(8,128)} %constant.5.clone.gather_ref) | copy-start | bytes 20740
  46.2 34.5 %copy-start.8 = (s32[8,225]{1,0:T(8,128)S(1)}, s32[8,225]{1,0:T(8,128)}, u32[]{:S(2)}) copy-start(s32[8,225]{1,0:T(8,128)} %weights_ref.1) | copy-start | bytes 21604
  46.2 34.4 %all-to-all-start = ((f32[128,24,128]{2,1,0:T(8,128)}), f32[128,24,128]{2,1,0:T(8,128)S(1)}, u32[]{:S(2)}, u32[]{:S(2)}) async-start(f32[128,24,128]{2,1,0:T(8,128)} %bitcast.3), calls=%async_computation | async-start | bytes 3145728 | tf_op jit(solution)/shard_map/all_to_all | solution.py:512
  56.5 18.7 %collective-permute-start = (f32[3,256]{1,0:T(4,128)S(1)}, f32[3,256]{1,0:T(4,128)S(1)}, u32[]{:S(2)}, u32[]{:S(2)}) collective-permute-start(f32[3,256]{1,0:T(4,128)S(1)} %bitcast.16), channel_id=1, source_target_pairs={{1,0},{2,1},{3,2},{4,3},{5,4},{6,5},{7,6},{8,7},{9,8},{10,9},{11,1... | collective-permute-start | bytes 9224 | tf_op jit(solution)/shard_map/ppermute | solution.py:494
  83.0 7.6 %collective-permute-start.1 = (f32[3,256]{1,0:T(4,128)S(1)}, f32[3,256]{1,0:T(4,128)S(1)}, u32[]{:S(2)}, u32[]{:S(2)}) collective-permute-start(f32[3,256]{1,0:T(4,128)S(1)} %get-tuple-element.7), channel_id=1, source_target_pairs={{0,1},{1,2},{2,3},{3,4},{4,5},{5,6},{6,7},{7,8},{8,9},{9,10},{10,1... | collective-permute-start | bytes 9224 | tf_op jit(solution)/shard_map/ppermute | solution.py:494

commit v2 on v1

--- a/solution.py
+++ b/solution.py
@@ -12,8 +12,11 @@
 GX = 15
 NODES = 256
 CAP = 40
-DEVICES = 128
-ROWS = 24
+GROUPS = 8
+MEMBERS = 16
+DEVICES = GROUPS * MEMBERS
+CHUNKS = 4
+CHUNK_ROWS = 6
 FIXED_STEPS = float(2**20 - 1)
 
 SLIP_PLANES = [
@@ -92,10 +95,15 @@
     stack.append(value)
 
 
-def build_table(euler_ref, table_ref):
-    half_sum = 0.5 * (euler_ref[0] + euler_ref[2])
-    half_diff = 0.5 * (euler_ref[0] - euler_ref[2])
-    half_mid = 0.5 * euler_ref[1]
+def build_table(euler_ref, angle_ref, table_ref):
+    for angle in range(3):
+        for row in range(32):
+            angle_ref[angle, row : row + 1] = euler_ref[
+                angle : angle + 1, row * 128 : row * 128 + 128
+            ]
+    half_sum = 0.5 * (angle_ref[0] + angle_ref[2])
+    half_diff = 0.5 * (angle_ref[0] - angle_ref[2])
+    half_mid = 0.5 * angle_ref[1]
     cos_mid, sin_mid = jnp.cos(half_mid), jnp.sin(half_mid)
     real = cos_mid * jnp.cos(half_sum)
     flip = jnp.where(real < 0.0, -1.0, 1.0)
@@ -135,88 +143,53 @@
     return [qa * a, qb * b, qc * c, qa * b, qa * c, qb * c, lin * a, lin * b, lin * c]
 
 
+def octant_entries(terms, per_octant):
+    xx, yy, zz, xy, xz, yz, wx, wy, wz = terms
+    share = per_octant / 8.0
+    return [
+        share - (yy + zz),
+        xy - wz,
+        xz + wy,
+        xy + wz,
+        share - (xx + zz),
+        yz - wx,
+        xz - wy,
+        yz + wx,
+        share - (xx + yy),
+    ]
+
+
+def swapped(values, step, keep):
+    return jnp.where(keep, pltpu.roll(values, 8 - step, 0), pltpu.roll(values, step, 0))
+
+
 def sum_sublanes(parts, row):
+    half = len(parts) // 2
     low4 = row < 4
     level = [
-        jnp.where(low4, parts[q], parts[q + 4])
-        + pltpu.roll(jnp.where(low4, parts[q + 4], parts[q]), 4, 0)
-        for q in range(4)
+        jnp.where(low4, parts[n], parts[n + half])
+        + pltpu.roll(jnp.where(low4, parts[n + half], parts[n]), 4, 0)
+        for n in range(half)
     ]
     for step in (2, 1):
         keep = (row & step) == 0
-        merged = []
-        for q in range(step):
-            other = jnp.where(keep, level[q + step], level[q])
-            moved = jnp.where(keep, pltpu.roll(other, 8 - step, 0), pltpu.roll(other, step, 0))
-            merged.append(jnp.where(keep, level[q], level[q + step]) + moved)
-        level = merged
+        if len(level) == 1:
+            level = [level[0] + swapped(level[0], step, keep)]
+            continue
+        half = len(level) // 2
+        level = [
+            jnp.where(keep, level[n], level[n + half])
+            + swapped(jnp.where(keep, level[n + half], level[n]), step, keep)
+            for n in range(half)
+        ]
     return level[0]
 
 
-def octant_kernel(ids_ref, euler_ref, out_ref, table_ref, part_ref):
-    build_table(euler_ref, table_ref)
-    row = lax.broadcasted_iota(jnp.int32, (8, 128), 0)
-    tiles = ids_ref.shape[0] // 8
-    per_octant = ids_ref.shape[0] // 8
-
-    @pl.loop(0, ids_ref.shape[1] // 128)
-    def _(block):
-        columns = pl.ds(pl.multiple_of(block * 128, 128), 128)
-        sums = None
-        octant = 0
-        for t in range(tiles):
-            terms = rotation_terms(*lookup(table_ref, ids_ref[8 * t : 8 * t + 8, columns]))
-            end = (octant + 1) * per_octant
-            if 8 * t + 8 < end:
-                sums = terms if sums is None else [s + v for s, v in zip(sums, terms)]
-                continue
-            split = end - 8 * t
-            inside = row < split
-            head = terms if split == 8 else [jnp.where(inside, v, 0.0) for v in terms]
-            done = head if sums is None else [s + v for s, v in zip(sums, head)]
-            for n in range(9):
-                part_ref[n * 8 + octant] = done[n]
-            sums = None if split == 8 else [jnp.where(inside, 0.0, v) for v in terms]
-            octant += 1
-        xx, yy, zz, xy, xz, yz, wx, wy, wz = [
-            sum_sublanes([part_ref[n * 8 + q] for q in range(8)], row) for n in range(9)
-        ]
-        total = float(per_octant)
-        entries = [
-            total - (yy + zz),
-            xy - wz,
-            xz + wy,
-            xy + wz,
-            total - (xx + zz),
-            yz - wx,
-            xz - wy,
-            yz + wx,
-            total - (xx + yy),
-        ]
-        for n in range(9):
-            out_ref[n, :, columns] = entries[n]
-
-
-def octant_totals(grain_ids, euler_angles):
-    bricks = grain_ids.shape[1]
-    return pl.pallas_call(
-        octant_kernel,
-        out_shape=jax.ShapeDtypeStruct((9, 8, bricks), jnp.float32),
-        in_specs=[pl.BlockSpec(memory_space=pltpu.VMEM)] * 2,
-        out_specs=pl.BlockSpec(memory_space=pltpu.VMEM),
-        scratch_shapes=[
-            pltpu.VMEM((64, 8, 128), jnp.int32),
-            pltpu.VMEM((72, 8, 128), jnp.float32),
-        ],
-        compiler_params=pltpu.CompilerParams(vmem_limit_bytes=VMEM_LIMIT),
-        name="octant_totals",
-    )(grain_ids, euler_angles.reshape(3, 32, 128))
-
-
 NT_DIMS = (((1,), (1,)), ((), ()))
-
-
-def slot_kernel(total_ref, owner_ref, element_ref, active_ref, out_ref, pick_ref, slot_ref):
+MESH = pl.DeviceIdType.MESH
+
+
+def find_slots(owner_ref, element_ref, active_ref):
     span = 256
     device = lax.broadcasted_iota(jnp.int32, (DEVICES, span), 0)
     slot = lax.broadcasted_iota(jnp.int32, (CAP, span), 0)
@@ -228,8 +201,9 @@
     ones = jnp.ones((span, span), jnp.bfloat16)
     carry = jnp.zeros((DEVICES, span), jnp.float32)
     found = jnp.zeros((3 * CAP, DEVICES), jnp.float32)
-    for start in range(0, total_ref.shape[2], span):
-        owned = device == owner_ref[:, start : start + span]
+    for start in range(0, owner_ref.shape[1], span):
+        owner = owner_ref[:, start : start + span]
+        owned = device == ((owner & (MEMBERS - 1)) * GROUPS + jnp.right_shift(owner, 4))
         owned_half = owned.astype(jnp.bfloat16)
         earlier = carry + jnp.dot(owned_half, before, preferred_element_type=jnp.float32)
         carry = carry + jnp.dot(owned_half, ones, preferred_element_type=jnp.float32)
@@ -238,59 +212,293 @@
         label = jnp.where(
             active_ref[:, start : start + span] > 0, element_ref[:, start : start + span] + 1, 0
         )
-        values = [(brick + start) >> 7, (brick + start) & 127, label]
+        values = [jnp.right_shift(brick + start, 7), (brick + start) & 127, label]
         left = jnp.concatenate(
             [jnp.where(mine, value.astype(jnp.float32), 0.0) for value in values], axis=0
         ).astype(jnp.bfloat16)
         found = found + lax.dot_general(
             left, owned_half, NT_DIMS, preferred_element_type=jnp.float32
         )
+    return found
+
+
+def exchange_kernel(
+    ids_hbm,
+    euler_ref,
+    owner_ref,
+    element_ref,
+    active_ref,
+    below_ref,
+    sums_ref,
+    above_ref,
+    ids_ref,
+    angle_ref,
+    table_ref,
+    carry_ref,
+    total_ref,
+    pick_ref,
+    slot_ref,
+    out1_ref,
+    in1_ref,
+    out2_ref,
+    in2_ref,
+    got_ref,
+    land_ref,
+    ids_sem,
+    send1_sem,
+    recv1_sem,
+    send2_sem,
+    recv2_sem,
+    layer_sem,
+):
+    ca, fe = lax.axis_index("ca"), lax.axis_index("fe")
+    barrier = pltpu.get_barrier_semaphore()
+
+    def member(i):
+        return lax.rem(fe + i, MEMBERS)
+
+    def group(i):
+        return lax.rem(ca + i, GROUPS)
+
+    @pl.loop(1, MEMBERS)
+    def _(i):
+        pl.semaphore_signal(barrier, inc=1, device_id=(ca, member(i)), device_id_type=MESH)
+
+    @pl.loop(1, GROUPS)
+    def _(i):
+        pl.semaphore_signal(barrier, inc=1, device_id=(group(i), fe), device_id_type=MESH)
+
+    row = lax.broadcasted_iota(jnp.int32, (8, 128), 0)
+    cells = ids_hbm.shape[0]
+    per_octant = cells // 8
+    tiles = cells // 8
+    step_tiles = 7
+    blocks = ids_hbm.shape[1] // 128
+
+    def ids_copy(p):
+        rows = pl.ds(p * 8 * step_tiles, min(8 * step_tiles, cells - p * 8 * step_tiles))
+        return pltpu.make_async_copy(ids_hbm.at[rows], ids_ref.at[rows], ids_sem.at[p])
+
+    for p in range(CHUNKS):
+        ids_copy(p).start()
+
+    def hop1(p, i):
+        there = pl.ds(pl.multiple_of(member(i) * GROUPS, 8), GROUPS)
+        here = pl.ds(pl.multiple_of(fe * GROUPS, 8), GROUPS)
+        return pltpu.make_async_remote_copy(
+            src_ref=out1_ref.at[p, :, there],
+            dst_ref=in1_ref.at[p, :, here],
+            send_sem=send1_sem.at[p, i],
+            recv_sem=recv1_sem.at[p, i],
+            device_id=(ca, member(i)),
+            device_id_type=MESH,
+        )
+
+    def hop2(p, i):
+        there = pl.ds(pl.multiple_of(group(i) * MEMBERS, 8), MEMBERS)
+        here = pl.ds(pl.multiple_of(ca * MEMBERS, 8), MEMBERS)
+        return pltpu.make_async_remote_copy(
+            src_ref=out2_ref.at[p, :, there],
+            dst_ref=in2_ref.at[p, :, here],
+            send_sem=send2_sem.at[p, i],
+            recv_sem=recv2_sem.at[p, i],
+            device_id=(group(i), fe),
+            device_id_type=MESH,
+        )
+
+    def layer_copy():
+        return pltpu.make_async_remote_copy(
+            src_ref=below_ref,
+            dst_ref=land_ref,
+            send_sem=layer_sem.at[0],
+            recv_sem=layer_sem.at[1],
+            device_id=(ca, lax.rem(fe + MEMBERS - 1, MEMBERS)),
+            device_id_type=MESH,
+        )
+
+    def start1(p):
+        @pl.loop(1, MEMBERS)
+        def _(i):
+            hop1(p, i).start()
+
+        here = pl.ds(pl.multiple_of(fe * GROUPS, 8), GROUPS)
+        in1_ref[p, :, here] = out1_ref[p, :, here]
+
+    def pass_on(p):
+        @pl.loop(1, MEMBERS)
+        def _(i):
+            hop1(p, i).wait_recv()
+
+        for c in range(CHUNK_ROWS):
+            for g in range(GROUPS):
+                out2_ref[p, c, g * MEMBERS : g * MEMBERS + MEMBERS] = in1_ref[
+                    p, c, pl.ds(g, MEMBERS, stride=GROUPS), :
+                ]
+
+        @pl.loop(1, GROUPS)
+        def _(i):
+            hop2(p, i).start()
+
+        here = pl.ds(pl.multiple_of(ca * MEMBERS, 8), MEMBERS)
+        in2_ref[p, :, here] = out2_ref[p, :, here]
+
+    def take_in(p):
+        @pl.loop(1, GROUPS)
+        def _(i):
+            hop2(p, i).wait_recv()
+
+        for c in range(CHUNK_ROWS):
+            got_ref[p, c * 128 : c * 128 + 128] = in2_ref[p, c].T
+
+    build_table(euler_ref, angle_ref, table_ref)
+    found = find_slots(owner_ref, element_ref, active_ref)
     pick_ref[...] = found[: 2 * CAP].astype(jnp.int32)
-    words = 72 * CAP
-    slot_ref[words : words + CAP] = found[2 * CAP :]
-    slot_ref[words + CAP :] = jnp.zeros((slot_ref.shape[0] - words - CAP, 128), jnp.float32)
-    blocks = total_ref.shape[2] // 128
+    got_ref[:, CHUNK_ROWS * 128 :] = jnp.zeros(
+        (CHUNKS, got_ref.shape[1] - CHUNK_ROWS * 128, 128), jnp.float32
+    )
     depth = blocks.bit_length() - 1
-    tiles = CAP // 8
-
-    @pl.loop(0, 9)
-    def _(entry):
-        for t in range(tiles):
-            lanes = pick_ref[CAP + 8 * t : CAP + 8 * t + 8]
-            high = pick_ref[8 * t : 8 * t + 8]
+
+    for p in range(CHUNKS):
+        ids_copy(p).wait()
+
+        @pl.loop(0, blocks)
+        def _(block, p=p):
+            columns = pl.ds(pl.multiple_of(block * 128, 128), 128)
+            octant = 2 * p
+            sums = None if p == 0 else [carry_ref[block, n] for n in range(9)]
+            entries = []
+            for t in range(step_tiles * p, min(step_tiles * p + step_tiles, tiles)):
+                terms = rotation_terms(*lookup(table_ref, ids_ref[8 * t : 8 * t + 8, columns]))
+                end = (octant + 1) * per_octant
+                if 8 * t + 8 < end:
+                    sums = terms if sums is None else [s + v for s, v in zip(sums, terms)]
+                    continue
+                split = end - 8 * t
+                inside = row < split
+                head = terms if split == 8 else [jnp.where(inside, v, 0.0) for v in terms]
+                done = head if sums is None else [s + v for s, v in zip(sums, head)]
+                entries.append(octant_entries(done, per_octant))
+                sums = None if split == 8 else [jnp.where(inside, 0.0, v) for v in terms]
+                octant += 1
+            if sums is not None:
+                for n in range(9):
+                    carry_ref[block, n] = sums[n]
+            parts = [entries[n & 1][n >> 1] for n in range(18)]
+            for n in range(3):
+                total_ref[n, :, columns] = sum_sublanes(parts[8 * n : 8 * n + 8], row)
+
+        @pl.loop(0, CAP // 8)
+        def _(t):
+            lanes = pick_ref[pl.ds(pl.multiple_of(CAP + 8 * t, 8), 8)]
+            high = pick_ref[pl.ds(pl.multiple_of(8 * t, 8), 8)]
             bits = [(high & (1 << level)) != 0 for level in range(depth)]
-            for q in range(8):
+            for m in range(18):
+                line = m % 8 if m < 16 else 4 * (m - 16)
                 stack = []
                 for block in range(blocks):
                     values = jnp.broadcast_to(
-                        total_ref[entry, q : q + 1, block * 128 : block * 128 + 128], (8, 128)
+                        total_ref[m // 8, line : line + 1, block * 128 : block * 128 + 128],
+                        (8, 128),
                     )
                     merge_tree(stack, lane_pick(values, lanes), block, bits)
-                row = pl.multiple_of((entry * 8 + q) * CAP + 8 * t, 8)
-                slot_ref[pl.ds(row, 8), :] = stack[0]
-
-    for c in range(ROWS):
-        if c < slot_ref.shape[0] // 128:
-            flipped = slot_ref[c * 128 : c * 128 + 128].T
-        else:
-            flipped = jnp.zeros((128, 128), jnp.float32)
-        out_ref[pl.ds(c, DEVICES, stride=ROWS), :] = flipped
-
-
-def slots_to_send(totals, owner, element, active):
-    bricks = totals.shape[2]
+                slot_ref[pl.ds(pl.multiple_of(m * CAP + 8 * t, 8), 8), :] = stack[0]
+
+        if p == 0:
+            slot_ref[18 * CAP : 19 * CAP] = found[2 * CAP :]
+            slot_ref[19 * CAP :] = jnp.zeros((slot_ref.shape[0] - 19 * CAP, 128), jnp.float32)
+        for c in range(CHUNK_ROWS):
+            out1_ref[p, c] = slot_ref[c * 128 : c * 128 + 128].T
+        if p == 0:
+            pl.semaphore_wait(barrier, MEMBERS + GROUPS - 2)
+            layer_copy().start()
+        start1(p)
+        if p >= 1:
+            pass_on(p - 1)
+        if p >= 2:
+            take_in(p - 2)
+
+    layer_copy().wait()
+    above_ref[...] = jnp.where(fe == MEMBERS - 1, 0.0, land_ref[...])
+    pass_on(CHUNKS - 1)
+    take_in(CHUNKS - 2)
+    take_in(CHUNKS - 1)
+    got_ref[0, 19 * CAP : 20 * CAP] = jnp.ones((CAP, 128), jnp.float32)
+
+    label_value = lax.broadcasted_iota(jnp.int32, (NODES, 128), 0).astype(jnp.float32) + 1.0
+    sums = jnp.zeros((8 * 24, NODES), jnp.float32)
+    for r in range(0, CAP, 2):
+        left, right = [], []
+        for n in (r, r + 1):
+            values = jnp.concatenate(
+                [got_ref[p, pl.ds(n, 24, stride=CAP), :] for p in range(CHUNKS)], axis=0
+            )
+            high = values.astype(jnp.bfloat16).astype(jnp.float32)
+            left.append(jnp.concatenate([high, values - high], axis=0).astype(jnp.bfloat16))
+            hit = label_value == got_ref[0, 18 * CAP + n : 18 * CAP + n + 1, :]
+            right.append(hit.astype(jnp.bfloat16))
+        sums = sums + lax.dot_general(
+            jnp.concatenate(left, axis=1),
+            jnp.concatenate(right, axis=1),
+            NT_DIMS,
+            preferred_element_type=jnp.float32,
+        )
+    sums_ref[...] = sums[:96] + sums[96:]
+    for p in range(CHUNKS):
+
+        @pl.loop(1, MEMBERS)
+        def _(i, p=p):
+            hop1(p, i).wait_send()
+
+        @pl.loop(1, GROUPS)
+        def _(i, p=p):
+            hop2(p, i).wait_send()
+
+
+def exchanged_sums(grain_ids, euler_angles, owner, element, active, below):
+    bricks = grain_ids.shape[1]
+    hop = pltpu.VMEM((CHUNKS, CHUNK_ROWS, DEVICES, 128), jnp.float32)
+    vmem = pl.BlockSpec(memory_space=pltpu.VMEM)
     return pl.pallas_call(
-        slot_kernel,
-        out_shape=jax.ShapeDtypeStruct((DEVICES * ROWS, 128), jnp.float32),
-        in_specs=[pl.BlockSpec(memory_space=pltpu.VMEM)] * 4,
-        out_specs=pl.BlockSpec(memory_space=pltpu.VMEM),
+        exchange_kernel,
+        out_shape=(
+            jax.ShapeDtypeStruct((96, NODES), jnp.float32),
+            jax.ShapeDtypeStruct((3, NODES), jnp.float32),
+        ),
+        in_specs=[pl.BlockSpec(memory_space=pl.ANY)] + [vmem] * 5,
+        out_specs=(vmem, vmem),
         scratch_shapes=[
+            pltpu.VMEM(grain_ids.shape, jnp.int32),
+            pltpu.VMEM((3, 32, 128), jnp.float32),
+            pltpu.VMEM((64, 8, 128), jnp.int32),
+            pltpu.VMEM((bricks // 128, 9, 8, 128), jnp.float32),
+            pltpu.VMEM((3, 8, bricks), jnp.float32),
             pltpu.VMEM((2 * CAP, 128), jnp.int32),
-            pltpu.VMEM(((ROWS - 1) * 128, 128), jnp.float32),
+            pltpu.VMEM((CHUNK_ROWS * 128, 128), jnp.float32),
+            hop,
+            hop,
+            hop,
+            hop,
+            pltpu.VMEM((CHUNKS, 24 * CAP, 128), jnp.float32),
+            pltpu.VMEM((3, NODES), jnp.float32),
+            pltpu.SemaphoreType.DMA((CHUNKS,)),
+            pltpu.SemaphoreType.DMA((CHUNKS, MEMBERS)),
+            pltpu.SemaphoreType.DMA((CHUNKS, MEMBERS)),
+            pltpu.SemaphoreType.DMA((CHUNKS, GROUPS)),
+            pltpu.SemaphoreType.DMA((CHUNKS, GROUPS)),
+            pltpu.SemaphoreType.DMA((2,)),
         ],
-        compiler_params=pltpu.CompilerParams(vmem_limit_bytes=VMEM_LIMIT),
-        name="slots_to_send",
-    )(totals, owner.reshape(1, bricks), element.reshape(1, bricks), active.reshape(1, bricks))
+        compiler_params=pltpu.CompilerParams(
+            vmem_limit_bytes=VMEM_LIMIT, collective_id=0, has_side_effects=True
+        ),
+        name="exchanged_sums",
+    )(
+        grain_ids,
+        euler_angles,
+        owner.reshape(1, bricks),
+        element.reshape(1, bricks),
+        active.reshape(1, bricks),
+        below,
+    )
 
 
 def split_three(values):
@@ -307,7 +515,7 @@
 
 
 def element_kernel(
-    got_ref,
+    sums_ref,
     below_ref,
     above_ref,
     stress_ref,
@@ -318,35 +526,14 @@
     stress_out,
     owned_out,
     top_out,
-    slot_ref,
 ):
     elements = stress_ref.shape[2]
-    for c in range(ROWS - 1):
-        slot_ref[c * 128 : c * 128 + 128] = got_ref[pl.ds(c, DEVICES, stride=ROWS), :].T
-    sums = jnp.zeros((160, NODES), jnp.float32)
-    label_value = lax.broadcasted_iota(jnp.int32, (NODES, 128), 0).astype(jnp.float32) + 1.0
-    ones = jnp.ones((16, 128), jnp.bfloat16)
-    for r in range(0, CAP, 2):
-        left, right = [], []
-        for n in (r, r + 1):
-            values = slot_ref[pl.ds(n, 72, stride=CAP), :]
-            high = values.astype(jnp.bfloat16).astype(jnp.float32)
-            left.append(
-                jnp.concatenate(
-                    [jnp.concatenate([high, values - high], axis=0).astype(jnp.bfloat16), ones],
-                    axis=0,
-                )
-            )
-            hit = label_value == slot_ref[72 * CAP + n : 72 * CAP + n + 1]
-            right.append(hit.astype(jnp.bfloat16))
-        sums = sums + lax.dot_general(
-            jnp.concatenate(left, axis=1),
-            jnp.concatenate(right, axis=1),
-            NT_DIMS,
-            preferred_element_type=jnp.float32,
-        )
-    counts = sums[144:145]
-    orient = (sums[:72] + sums[72:144]) / (8.0 * jnp.maximum(counts, 1.0))
+    counts = sums_ref[19:20, :]
+    weight = 1.0 / (8.0 * jnp.maximum(counts, 1.0))
+    frames = []
+    for n in range(9):
+        lines = [sums_ref[24 * p + 2 * n : 24 * p + 2 * n + 2, :] for p in range(CHUNKS)]
+        frames.append((jnp.concatenate(lines, axis=0) * weight)[:, :elements])
 
     node = lax.broadcasted_iota(jnp.int32, (NODES, NODES), 0)
     lane = lax.broadcasted_iota(jnp.int32, (NODES, NODES), 1)
@@ -397,8 +584,7 @@
         trial.append(stress_ref[component] + change)
 
     def frame(i, j):
-        n = (i * 3 + j) * 8
-        return orient[n : n + 8, :elements]
+        return frames[i * 3 + j]
 
     def rotated(vector):
         out = []
@@ -465,7 +651,7 @@
             out[comp : comp + 1, :] = line
 
 
-def element_update(got, below, above, stress_old, resistance, quad_weights):
+def element_update(sums, below, above, stress_old, resistance, quad_weights):
     grads, forces = gradient_matrices()
     layer = jax.ShapeDtypeStruct((3, NODES), jnp.float32)
     return pl.pallas_call(
@@ -473,11 +659,10 @@
         out_shape=(jax.ShapeDtypeStruct(stress_old.shape, jnp.float32), layer, layer),
         in_specs=[pl.BlockSpec(memory_space=pltpu.VMEM)] * 8,
         out_specs=(pl.BlockSpec(memory_space=pltpu.VMEM),) * 3,
-        scratch_shapes=[pltpu.VMEM(((ROWS - 1) * 128, 128), jnp.float32)],
         compiler_params=pltpu.CompilerParams(vmem_limit_bytes=VMEM_LIMIT),
         name="element_update",
     )(
-        got,
+        sums,
         below,
         above,
         stress_old,
@@ -506,14 +691,11 @@
     quad_weights,
 ):
     below = displacement[:, 0]
-    above = passed_along(below, "fe", -1)
-    totals = octant_totals(grain_ids, euler_angles)
-    send = slots_to_send(totals, brick_owner, brick_element, brick_active)
-    got = lax.all_to_all(
-        send.reshape(DEVICES, ROWS, 128), ("ca", "fe"), split_axis=0, concat_axis=0, tiled=True
+    sums, above = exchanged_sums(
+        grain_ids, euler_angles, brick_owner, brick_element, brick_active, below
     )
     stress_new, owned, top = element_update(
-        got.reshape(DEVICES * ROWS, 128), below, above, stress_old, resistance, quad_weights
+        sums, below, above, stress_old, resistance, quad_weights
     )
     forces = owned + passed_along(top, "fe", 1)
     return (stress_new, forces[:, None])

time: 91.5 us -> 84.3 us (0.921)
  Pallas kernels: 45.5 us -> 69.9 us
  waiting for transfers between devices: 24.6 us -> 5.43 us
  starting transfers between devices: 17.4 us -> 2.16 us
  local copies, waits for them, and re-layouts: 2.96 us -> 5.7 us
    pallas_call x2 -> x1, Pallas kernels: 43.1 us -> 68.7 us  [exchanged_sums(): pl.pallas_call(exchange_kernel, out_shape=(jax.ShapeDtypeStruct((96, NODE...]
    ppermute x2 -> x1, waiting for transfers between devices: 19.1 us -> 5.43 us  [passed_along(): return lax.ppermute(block, axis, route)]
    all_to_all x1 -> x0, starting transfers between devices: 10.2 us -> none  [body(): lax.all_to_all(send.reshape(DEVICES, ROWS, 128), ('ca', 'fe'), split_axis...]
    all_to_all x1 -> x0, waiting for transfers between devices: 5.43 us -> none  [body(): lax.all_to_all(send.reshape(DEVICES, ROWS, 128), ('ca', 'fe'), split_axis...]
    ppermute x2 -> x1, starting transfers between devices: 7.17 us -> 2.16 us  [passed_along(): return lax.ppermute(block, axis, route)]
    unnamed x23 -> x22, local copies, waits for them, and re-layouts: 2.96 us -> 5.7 us
    pallas_call x1, Pallas kernels: 2.38 us -> 1.21 us  [element_update(): pl.pallas_call(element_kernel, out_shape=(jax.ShapeDtypeStruct(stress_old...]
  transfers between devices with their start and end apart: 3 -> 1, of which waited for: 3 -> 1; matrix products, arithmetic and copies ran while one was open for 0% -> 0% of each run, Pallas kernels for 0% -> 0%
where the time goes in v2:
time: 84.3 us; the launch traced here: 83.9 us
  Pallas kernels  69.9 us (83%)
  local copies, waits for them, and re-layouts  5.7 us (7%)
  waiting for transfers between devices  5.43 us (6%)
  starting transfers between devices  2.16 us (3%)
    pallas_call x1, Pallas kernels, exchanged_sums(): pl.pallas_call(exchange_kernel, out_shape=(jax.ShapeDtypeStruct((96, NODE...  68.7 us
    unnamed x22, local copies, waits for them, and re-layouts  5.7 us
    ppermute x1, waiting for transfers between devices, passed_along(): return lax.ppermute(block, axis, route)  5.43 us
    ppermute x1, starting transfers between devices, passed_along(): return lax.ppermute(block, axis, route)  2.16 us
  transfers between devices with their start and end apart: 1, of which 1 were waited for; matrix products, arithmetic and copies ran while one was open for 0% of the time, Pallas kernels for 0%

profile of v2, /device:TPU:32, one launch (start us, length us, event | category | flops | bytes accessed | tf_op | source)
XLA Modules:
  0.0 83.9 jit_solution(267265440194543732)
XLA Ops:
  0.6 0.0 copy-start.5
  0.6 0.7 copy.16
  1.3 0.0 copy-start
  1.3 1.5 %copy-done = s32[216,2048]{1,0:T(8,128)S(1)} copy-done((s32[216,2048]{1,0:T(8,128)S(1)}, s32[216,2048]{1,0:T(8,128)}, u32[]{:S(2)}) %copy-start) | copy-done | bytes 1769496
  2.8 0.0 copy-start.2
  2.8 0.8 copy-done.2
  3.7 0.0 copy-start.6
  3.7 0.7 copy-done.6
  4.3 0.0 copy-start.7
  4.4 0.7 copy-done.7
  5.0 0.0 copy-start.8
  5.0 0.7 copy-done.8
  5.7 0.0 copy-start.1
  5.7 0.0 copy-start.3
  5.8 68.7 %exchanged_sums.1 = (f32[96,256]{1,0:T(8,128)S(1)}, f32[3,256]{1,0:T(4,128)S(1)}) custom-call(s32[216,2048]{1,0:T(8,128)S(1)} %copy-done, f32[3,4096]{1,0:T(4,128)S(1)} %copy-done.2, s32[1,2048]{1,0:T(1,128)S(1)} %bitcast.10, s32[1,2048]{1,0:T(1,128)S(1)} %bitcast.11, s32[1,2048]{1,0:T(1,128)S(1)} %bitcast.12, f32[3,256]{1,0:T(4,128)S(1)} %bitcast.8), custom_call_target="tpu_custom_call" | custom-call | tf_op jit(solution)/shard_map/exchanged_sums/pallas_call | solution.py:461
  74.5 0.0 copy-done.5
  74.5 0.0 copy-done.1
  74.5 0.0 copy-done.3
  74.5 0.0 copy-done.4
  74.5 0.0 copy-done.9
  74.5 1.2 %element_update.1 = (f32[6,8,225]{2,1,0:T(8,128)}, f32[3,256]{1,0:T(4,128)S(1)}, f32[3,256]{1,0:T(4,128)S(1)}) custom-call(f32[96,256]{1,0:T(8,128)S(1)} %get-tuple-element.7.sums_ref, f32[3,256]{1,0:T(4,128)S(1)} %bitcast.9, f32[3,256]{1,0:T(4,128)S(1)} %get-tuple-element.8.above_ref, f32[6,8,225]{2,1,0:T(8,128)S(1)} %copy-done.3, ...), custom_call_target="tpu_custom_call" | custom-call | tf_op jit(solution)/shard_map/element_update/pallas_call | solution.py:657
  75.8 2.2 %collective-permute-start = (f32[3,256]{1,0:T(4,128)S(1)}, f32[3,256]{1,0:T(4,128)S(1)}, u32[]{:S(2)}, u32[]{:S(2)}) collective-permute-start(f32[3,256]{1,0:T(4,128)S(1)} %get-tuple-element.11), channel_id=1, source_target_pairs={{0,1},{1,2},{2,3},{3,4},{4,5},{5,6},{6,7},{7,8},{8,9},{9,10},{10,1... | collective-permute-start | bytes 9224 | tf_op jit(solution)/shard_map/ppermute | solution.py:679
  77.9 5.4 %collective-permute-done = f32[3,256]{1,0:T(4,128)S(1)} collective-permute-done((f32[3,256]{1,0:T(4,128)S(1)}, f32[3,256]{1,0:T(4,128)S(1)}, u32[]{:S(2)}, u32[]{:S(2)}) %collective-permute-start) | collective-permute-done | bytes 3104 | tf_op jit(solution)/shard_map/ppermute | solution.py:679
  83.4 0.6 copy.13
  (3 shorter events, 0.0 us)
Async XLA Ops:
  0.6 73.9 %copy-start.5 = (f32[24,72]{1,0:T(8,128)S(1)}, f32[24,72]{1,0:T(8,128)}, u32[]{:S(2)}) copy-start(f32[24,72]{1,0:T(8,128)} %constant.5.clone.gather_ref) | copy-start | bytes 20740
  1.3 1.5 %copy-start = (s32[216,2048]{1,0:T(8,128)S(1)}, s32[216,2048]{1,0:T(8,128)}, u32[]{:S(2)}) copy-start(s32[216,2048]{1,0:T(8,128)} %ids_hbm.1) | copy-start | bytes 5308420
  2.8 0.8 %copy-start.2 = (f32[3,4096]{1,0:T(4,128)S(1)}, f32[3,4096]{1,0:T(4,128)}, u32[]{:S(2)}) copy-start(f32[3,4096]{1,0:T(4,128)} %euler_ref.1) | copy-start | bytes 147460
  3.7 0.7 copy-start.6
  4.3 0.7 copy-start.7
  5.0 0.7 copy-start.8
  5.7 68.8 %copy-start.1 = (f32[12,8,225]{2,1,0:T(8,128)S(1)}, f32[12,8,225]{2,1,0:T(8,128)}, u32[]{:S(2)}) copy-start(f32[12,8,225]{2,1,0:T(8,128)} %resistance_ref.1) | copy-start | bytes 259204
  5.7 68.8 %copy-start.3 = (f32[6,8,225]{2,1,0:T(8,128)S(1)}, f32[6,8,225]{2,1,0:T(8,128)}, u32[]{:S(2)}) copy-start(f32[6,8,225]{2,1,0:T(8,128)} %stress_ref.1) | copy-start | bytes 129604
  5.7 68.8 %copy-start.4 = (f32[72,24]{1,0:T(8,128)S(1)}, f32[72,24]{1,0:T(8,128)}, u32[]{:S(2)}) copy-start(f32[72,24]{1,0:T(8,128)} %constant.4.clone.grads_ref) | copy-start | bytes 20740
  5.7 68.8 %copy-start.9 = (s32[8,225]{1,0:T(8,128)S(1)}, s32[8,225]{1,0:T(8,128)}, u32[]{:S(2)}) copy-start(s32[8,225]{1,0:T(8,128)} %weights_ref.1) | copy-start | bytes 21604
  75.8 7.6 %collective-permute-start = (f32[3,256]{1,0:T(4,128)S(1)}, f32[3,256]{1,0:T(4,128)S(1)}, u32[]{:S(2)}, u32[]{:S(2)}) collective-permute-start(f32[3,256]{1,0:T(4,128)S(1)} %get-tuple-element.11), channel_id=1, source_target_pairs={{0,1},{1,2},{2,3},{3,4},{4,5},{5,6},{6,7},{7,8},{8,9},{9,10},{10,1... | collective-permute-start | bytes 9224 | tf_op jit(solution)/shard_map/ppermute | solution.py:679

commit v3 on v1

v3 whole, which is shorter than its diff:
```python
import functools
import math

import jax
import jax.numpy as jnp
import numpy as np
from jax import lax
from jax.experimental import pallas as pl
from jax.experimental.pallas import tpu as pltpu
from jax.sharding import PartitionSpec as P

GX = 15
NODES = 256
CAP = 40
GROUPS = 8
MEMBERS = 16
DEVICES = GROUPS * MEMBERS
FIXED_STEPS = float(2**20 - 1)

SLIP_PLANES = [
    [value / math.sqrt(3.0) for value in row]
    for row in [[1, 1, 1]] * 3 + [[-1, 1, 1]] * 3 + [[1, -1, 1]] * 3 + [[1, 1, -1]] * 3
]
SLIP_DIRECTIONS = [
    [value / math.sqrt(2.0) for value in row]
    for row in [
        [0, 1, -1],
        [1, 0, -1],
        [1, -1, 0],
        [0, 1, -1],
        [1, 0, 1],
        [1, 1, 0],
        [0, 1, 1],
        [1, 0, -1],
        [1, 1, 0],
        [0, 1, 1],
        [1, 0, 1],
        [1, -1, 0],
    ]
]
LAMBDA_ELASTIC = 1.5
SHEAR_MODULUS = 1.0
RATE_STEP = 0.1
FIXED_POINT = 65536.0
EXCHANGE_VMEM = 63 << 20


def shape_gradients():
    grad_table = np.zeros((8, 8, 3))
    point_offset = 1.0 / math.sqrt(3.0)
    for quadrature in range(8):
        natural = [
            (2 * (quadrature >> shift_bits & 1) - 1) * point_offset for shift_bits in (2, 1, 0)
        ]
        for corner in range(8):
            sign_list = [2 * (corner >> shift_bits & 1) - 1 for shift_bits in (2, 1, 0)]
            factors = [1.0 + sign_list[axis_id] * natural[axis_id] for axis_id in range(3)]
            for direction in range(3):
                others = 1.0
                for axis_id in range(3):
                    if axis_id != direction:
                        others = others * factors[axis_id]
                grad_table[quadrature, corner, direction] = (
                    2.0 * sign_list[direction] * others / 8.0
                )
    return grad_table


def gradient_matrices():
    table = shape_gradients()
    grads = np.zeros((72, 24), np.float32)
    forces = np.zeros((24, 72), np.float32)
    for comp in range(3):
        for direction in range(3):
            for q in range(8):
                for corner in range(8):
                    value = table[q, corner, direction]
                    grads[(comp * 3 + direction) * 8 + q, comp * 8 + corner] = value
                    forces[comp * 8 + corner, (comp * 3 + direction) * 8 + q] = value
    return grads, forces


def lane_pick(row, lanes):
    return jnp.take_along_axis(row, lanes, axis=1, mode="promise_in_bounds")


def merge_tree(stack, value, index, bits):
    level = 0
    while index & 1:
        value = jnp.where(bits[level], value, stack.pop())
        level += 1
        index >>= 1
    stack.append(value)


def build_table(euler_ref, angle_ref, table_ref):
    for angle in range(3):
        for row in range(32):
            angle_ref[angle, row : row + 1] = euler_ref[
                angle : angle + 1, row * 128 : row * 128 + 128
            ]
    half_sum = 0.5 * (angle_ref[0] + angle_ref[2])
    half_diff = 0.5 * (angle_ref[0] - angle_ref[2])
    half_mid = 0.5 * angle_ref[1]
    cos_mid, sin_mid = jnp.cos(half_mid), jnp.sin(half_mid)
    real = cos_mid * jnp.cos(half_sum)
    flip = jnp.where(real < 0.0, -1.0, 1.0)
    scale = flip * FIXED_STEPS / (1.0 + jnp.abs(real))
    first = jnp.round(sin_mid * jnp.cos(half_diff) * scale).astype(jnp.int32)
    second = jnp.round(sin_mid * jnp.sin(half_diff) * scale).astype(jnp.int32)
    third = jnp.round(cos_mid * jnp.sin(half_sum) * scale).astype(jnp.int32)
    word_a = jnp.left_shift(first, 11) | (jnp.right_shift(third, 10) & 0x7FF)
    word_b = jnp.left_shift(second, 11) | (third & 0x3FF)
    for row in range(32):
        table_ref[row] = jnp.broadcast_to(word_a[row : row + 1], (8, 128))
        table_ref[32 + row] = jnp.broadcast_to(word_b[row : row + 1], (8, 128))


def lookup(table_ref, ids):
    lanes = ids & 127
    bits = [(ids & (128 << level)) != 0 for level in range(5)]
    words = ([], [])
    for row in range(32):
        for n, stack in enumerate(words):
            merge_tree(stack, lane_pick(table_ref[n * 32 + row], lanes), row, bits)
    return words[0][0], words[1][0]


def rotation_terms(word_a, word_b):
    a = jnp.right_shift(word_a, 11).astype(jnp.float32)
    b = jnp.right_shift(word_b, 11).astype(jnp.float32)
    c_bits = jnp.right_shift(jnp.left_shift(word_a, 21), 11) | (word_b & 0x3FF)
    c = c_bits.astype(jnp.float32)
    unit = 1.0 / FIXED_STEPS
    square = (a * a + b * b + c * c) * (unit * unit)
    inverse = 1.0 / (1.0 + square)
    inverse_square = inverse * inverse
    quad = inverse_square * (8.0 * unit * unit)
    lin = inverse_square * ((1.0 - square) * (4.0 * unit))
    qa, qb, qc = quad * a, quad * b, quad * c
    return [qa * a, qb * b, qc * c, qa * b, qa * c, qb * c, lin * a, lin * b, lin * c]


def octant_entries(terms, per_octant):
    xx, yy, zz, xy, xz, yz, wx, wy, wz = terms
    share = per_octant / 8.0
    return [
        share - (yy + zz),
        xy - wz,
        xz + wy,
        xy + wz,
        share - (xx + zz),
        yz - wx,
        xz - wy,
        yz + wx,
        share - (xx + yy),
    ]


def swapped(values, step, keep):
    return jnp.where(keep, pltpu.roll(values, 8 - step, 0), pltpu.roll(values, step, 0))


def sum_sublanes(parts, row):
    half = len(parts) // 2
    low4 = row < 4
    level = [
        jnp.where(low4, parts[n], parts[n + half])
        + pltpu.roll(jnp.where(low4, parts[n + half], parts[n]), 4, 0)
        for n in range(half)
    ]
    for step in (2, 1):
        keep = (row & step) == 0
        if len(level) == 1:
            level = [level[0] + swapped(level[0], step, keep)]
            continue
        half = len(level) // 2
        level = [
            jnp.where(keep, level[n], level[n + half])
            + swapped(jnp.where(keep, level[n + half], level[n]), step, keep)
            for n in range(half)
        ]
    return level[0]


NT_DIMS = (((1,), (1,)), ((), ()))
MESH = pl.DeviceIdType.MESH
OCTANTS = 8
CHUNKS = ((0, 2), (2, 4), (4, 6), (6, 7), (7, 8))
UNROLL = 4
WORDS = 384
ENTRY_ROWS = 8 * CAP
LABEL_ROWS = 368


def find_slots(owner_ref, element_ref, active_ref, owned_ref, rank_ref, single_ref, label_ref):
    span = 256
    device = lax.broadcasted_iota(jnp.int32, (DEVICES, span), 0)
    before = (
        lax.broadcasted_iota(jnp.int32, (span, span), 0)
        < lax.broadcasted_iota(jnp.int32, (span, span), 1)
    ).astype(jnp.bfloat16)
    ones = jnp.ones((span, span), jnp.bfloat16)
    slot = lax.broadcasted_iota(jnp.int32, (48, span), 0).astype(jnp.float32)
    carry = jnp.zeros((DEVICES, span), jnp.float32)
    for start in range(0, owner_ref.shape[1], span):
        owner = owner_ref[:, start : start + span]
        owned = device == ((owner & (MEMBERS - 1)) * GROUPS + jnp.right_shift(owner, 4))
        owned_half = owned.astype(jnp.bfloat16)
        earlier = carry + jnp.dot(owned_half, before, preferred_element_type=jnp.float32)
        carry = carry + jnp.dot(owned_half, ones, preferred_element_type=jnp.float32)
        rank = jnp.sum(jnp.where(owned, earlier, 0.0), axis=0, keepdims=True)
        label = jnp.where(
            active_ref[:, start : start + span] > 0, element_ref[:, start : start + span] + 1, 0
        ).astype(jnp.float32)
        single = jnp.where(slot == rank, 1.0, 0.0)
        labels = (single * label).astype(jnp.bfloat16)
        single = single.astype(jnp.bfloat16)
        eight = jnp.broadcast_to(rank, (8, span))
        for half in range(span // 128):
            lanes = slice(half * 128, half * 128 + 128)
            block = start // 128 + half
            place = (block % UNROLL) * 256
            owned_ref[block // UNROLL, :, place : place + 128] = owned_half[:, lanes]
            owned_ref[block // UNROLL, :, place + 128 : place + 256] = owned_half[:, lanes]
            single_ref[block] = single[:, lanes]
            label_ref[block] = labels[:, lanes]
            for pair in range(CAP // 2):
                both = [
                    jnp.where(eight[:, lanes] == float(2 * pair + n), 1.0, 0.0) for n in range(2)
                ]
                rank_ref[block, 16 * pair : 16 * pair + 16] = jnp.concatenate(
                    both, axis=0
                ).astype(jnp.bfloat16)


def halves(values):
    high = values.astype(jnp.bfloat16).astype(jnp.float32)
    out = []
    for part in (high, values - high):
        out.append(jnp.concatenate([part, part], axis=0).astype(jnp.bfloat16))
    return out


def split_three(values):
    high = values.astype(jnp.bfloat16)
    rest = values - high.astype(jnp.float32)
    mid = rest.astype(jnp.bfloat16)
    low = (rest - mid.astype(jnp.float32)).astype(jnp.bfloat16)
    return jnp.concatenate([high, mid, low], axis=0)


def joined_three(product):
    rows = product.shape[0] // 3
    return product[:rows] + product[rows : 2 * rows] + product[2 * rows :]


def element_places(elements):
    node = lax.broadcasted_iota(jnp.int32, (NODES, NODES), 0)
    lane = lax.broadcasted_iota(jnp.int32, (NODES, NODES), 1)
    base = lane
    for bound in range(GX, GX * GX, GX):
        base = base + jnp.where(lane >= bound, 1, 0)
    return ((node == base) & (lane < elements)).astype(jnp.bfloat16)


def trial_stress(below_ref, above_ref, stress_ref, grads_ref):
    elements = stress_ref.shape[2]
    to_element = element_places(elements)
    rows = []
    for comp in range(3):
        for corner in range(8):
            step_x, step_y, step_z = (corner >> 2 & 1, corner >> 1 & 1, corner & 1)
            source = above_ref if step_z else below_ref
            offset = step_y * (GX + 1) + step_x
            line = source[comp]
            rows.append(line if offset == 0 else pltpu.roll(line, NODES - offset, 1))
    corners = joined_three(
        jnp.dot(
            split_three(jnp.concatenate(rows, axis=0)),
            to_element,
            preferred_element_type=jnp.float32,
        )
    )
    gradients = jnp.dot(
        grads_ref[...],
        corners,
        precision=lax.Precision.HIGHEST,
        preferred_element_type=jnp.float32,
    )

    def grad(comp, direction):
        n = (comp * 3 + direction) * 8
        return gradients[n : n + 8, :elements]

    strain = [
        grad(0, 0),
        grad(1, 1),
        grad(2, 2),
        0.5 * (grad(1, 2) + grad(2, 1)),
        0.5 * (grad(0, 2) + grad(2, 0)),
        0.5 * (grad(0, 1) + grad(1, 0)),
    ]
    volume = strain[0] + strain[1] + strain[2]
    trial = []
    for component in range(6):
        change = 2.0 * SHEAR_MODULUS * strain[component]
        if component < 3:
            change = change + LAMBDA_ELASTIC * volume
        trial.append(stress_ref[component] + change)
    return trial


def stress_update(sums_ref, trial, resistance_ref):
    elements = resistance_ref.shape[2]
    weights = [1.0 / (8.0 * jnp.maximum(sums_ref[half, 72:73], 1.0)) for half in range(2)]
    frames = []
    for n in range(9):
        rows = pl.ds(n, OCTANTS, stride=8) if n < 8 else pl.ds(64, OCTANTS)
        parts = [sums_ref[half, rows, :] * weights[half] for half in range(2)]
        frames.append(jnp.concatenate(parts, axis=1)[:, :elements])

    def frame(i, j):
        return frames[i * 3 + j]

    def rotated(vector):
        out = []
        for i in range(3):
            terms = [float(vector[j]) * frame(i, j) for j in range(3) if vector[j] != 0.0]
            out.append(functools.reduce(lambda x, y: x + y, terms))
        return out

    normals = {tuple(vector): rotated(vector) for vector in SLIP_PLANES}
    correction = [jnp.zeros_like(trial[0]) for component in range(6)]
    for system in range(12):
        d = rotated(SLIP_DIRECTIONS[system])
        m = normals[tuple(SLIP_PLANES[system])]
        schmid = [
            d[0] * m[0],
            d[1] * m[1],
            d[2] * m[2],
            0.5 * (d[1] * m[2] + d[2] * m[1]),
            0.5 * (d[0] * m[2] + d[2] * m[0]),
            0.5 * (d[0] * m[1] + d[1] * m[0]),
        ]
        resolved = (
            trial[0] * schmid[0]
            + trial[1] * schmid[1]
            + trial[2] * schmid[2]
            + 2.0 * (trial[3] * schmid[3] + trial[4] * schmid[4] + trial[5] * schmid[5])
        )
        ratio = resolved / resistance_ref[system]
        slip_step = RATE_STEP * ratio * jnp.abs(ratio)
        correction = [
            correction[component] + slip_step * schmid[component] for component in range(6)
        ]
    updated = [
        trial[component] - 2.0 * SHEAR_MODULUS * correction[component] for component in range(6)
    ]
    return updated


def nodal_parts(updated, weights_ref, gather_ref):
    elements = weights_ref.shape[1]
    to_element = element_places(elements)
    scale = weights_ref[...].astype(jnp.float32) * (1.0 / (FIXED_POINT * 8.0))
    order = [0, 5, 4, 5, 1, 3, 4, 3, 2]
    pad = jnp.zeros((8, NODES - elements), jnp.float32)
    tensor = jnp.concatenate(
        [jnp.concatenate([updated[component] * scale, pad], axis=1) for component in order], axis=0
    )
    element_forces = jnp.dot(
        gather_ref[...],
        tensor,
        precision=lax.Precision.HIGHEST,
        preferred_element_type=jnp.float32,
    )
    placed = joined_three(
        lax.dot_general(
            split_three(element_forces), to_element, NT_DIMS, preferred_element_type=jnp.float32
        )
    )
    return placed


def layer_forces(placed, comp, step_z):
    line = jnp.zeros((1, NODES), jnp.float32)
    for corner in range(8):
        if (corner & 1) != step_z:
            continue
        offset = (corner >> 1 & 1) * (GX + 1) + (corner >> 2 & 1)
        part = placed[comp * 8 + corner : comp * 8 + corner + 1]
        line = line + (part if offset == 0 else pltpu.roll(part, offset, 1))
    return line


def exchange_kernel(
    ids_hbm,
    euler_hbm,
    owner_hbm,
    element_hbm,
    active_hbm,
    below_hbm,
    stress_hbm,
    resistance_hbm,
    weights_hbm,
    grads_hbm,
    gather_hbm,
    stress_out,
    forces_out,
    ids_ref,
    euler_ref,
    owner_ref,
    element_ref,
    active_ref,
    below_ref,
    angle_ref,
    table_ref,
    carry_ref,
    owned_ref,
    rank_ref,
    single_ref,
    label_ref,
    part_ref,
    wide_ref,
    acc_ref,
    out1_ref,
    in1_ref,
    out2_ref,
    in2_ref,
    got_ref,
    last_ref,
    sums_ref,
    stress_ref,
    resistance_ref,
    weights_ref,
    grads_ref,
    gather_ref,
    land_ref,
    above_ref,
    top_ref,
    under_ref,
    trial_ref,
    ids_sem,
    small_sem,
    send1_sem,
    recv1_sem,
    send2_sem,
    recv2_sem,
    layer_sem,
):
    ca, fe = lax.axis_index("ca"), lax.axis_index("fe")
    barrier = pltpu.get_barrier_semaphore()

    def member(i):
        return lax.rem(fe + i, MEMBERS)

    def group(i):
        return lax.rem(ca + i, GROUPS)

    row = lax.broadcasted_iota(jnp.int32, (8, 128), 0)
    cells = ids_hbm.shape[0]
    per_octant = cells // OCTANTS
    tiles = cells // 8
    blocks = ids_hbm.shape[1] // 128
    steps = blocks // UNROLL
    id_cuts = (0, 32, 56, 112, 168, 216)

    def ids_copy(n):
        rows = pl.ds(id_cuts[n], id_cuts[n + 1] - id_cuts[n])
        return pltpu.make_async_copy(ids_hbm.at[rows], ids_ref.at[rows], ids_sem.at[n])

    small = [
        pltpu.make_async_copy(source, target, small_sem.at[n])
        for n, (source, target) in enumerate(
            [
                (owner_hbm, owner_ref),
                (element_hbm, element_ref),
                (active_hbm, active_ref),
                (euler_hbm, euler_ref),
                (below_hbm, below_ref),
                (stress_hbm, stress_ref),
                (resistance_hbm, resistance_ref),
                (weights_hbm, weights_ref),
                (grads_hbm, grads_ref),
                (gather_hbm, gather_ref),
            ]
        )
    ]
    for copy in small[:5]:
        copy.start()
    for n in range(len(id_cuts) - 1):
        ids_copy(n).start()
    for copy in small[5:]:
        copy.start()

    @pl.loop(1, MEMBERS)
    def _(i):
        pl.semaphore_signal(barrier, inc=1, device_id=(ca, member(i)), device_id_type=MESH)

    @pl.loop(1, GROUPS)
    def _(i):
        pl.semaphore_signal(barrier, inc=1, device_id=(group(i), fe), device_id_type=MESH)

    def hop1(p, i):
        there = pl.ds(pl.multiple_of(member(i) * GROUPS, 8), GROUPS)
        here = pl.ds(pl.multiple_of(fe * GROUPS, 8), GROUPS)
        octants = pl.ds(CHUNKS[p][0], CHUNKS[p][1] - CHUNKS[p][0])
        return pltpu.make_async_remote_copy(
            src_ref=out1_ref.at[octants, :, there],
            dst_ref=in1_ref.at[octants, :, here],
            send_sem=send1_sem.at[p, i],
            recv_sem=recv1_sem.at[p, i],
            device_id=(ca, member(i)),
            device_id_type=MESH,
        )

    def hop2(p, i):
        there = pl.ds(pl.multiple_of(group(i) * MEMBERS, 8), MEMBERS)
        here = pl.ds(pl.multiple_of(ca * MEMBERS, 8), MEMBERS)
        octants = pl.ds(CHUNKS[p][0], CHUNKS[p][1] - CHUNKS[p][0])
        return pltpu.make_async_remote_copy(
            src_ref=out2_ref.at[octants, :, there],
            dst_ref=in2_ref.at[octants, :, here],
            send_sem=send2_sem.at[p, i],
            recv_sem=recv2_sem.at[p, i],
            device_id=(group(i), fe),
            device_id_type=MESH,
        )

    def layer_copy():
        return pltpu.make_async_remote_copy(
            src_ref=below_ref,
            dst_ref=land_ref,
            send_sem=layer_sem.at[0],
            recv_sem=layer_sem.at[1],
            device_id=(ca, lax.rem(fe + MEMBERS - 1, MEMBERS)),
            device_id_type=MESH,
        )

    def top_copy():
        return pltpu.make_async_remote_copy(
            src_ref=top_ref,
            dst_ref=under_ref,
            send_sem=layer_sem.at[2],
            recv_sem=layer_sem.at[3],
            device_id=(ca, member(1)),
            device_id_type=MESH,
        )

    def start1(p):
        if p == 0:
            pl.semaphore_wait(barrier, MEMBERS + GROUPS - 2)
            layer_copy().start()

        @pl.loop(1, MEMBERS)
        def _(i):
            hop1(p, i).start()

        here = pl.ds(pl.multiple_of(fe * GROUPS, 8), GROUPS)
        for q in range(*CHUNKS[p]):
            in1_ref[q, :, here] = out1_ref[q, :, here]

    def pass_on(p):
        @pl.loop(1, MEMBERS)
        def _(i):
            hop1(p, i).wait_recv()

        for q in range(*CHUNKS[p]):
            for c in range(WORDS // 128):
                for g in range(GROUPS):
                    out2_ref[q, c, g * MEMBERS : g * MEMBERS + MEMBERS] = in1_ref[
                        q, c, pl.ds(g, MEMBERS, stride=GROUPS), :
                    ]

        @pl.loop(1, GROUPS)
        def _(i):
            hop2(p, i).start()

        here = pl.ds(pl.multiple_of(ca * MEMBERS, 8), MEMBERS)
        for q in range(*CHUNKS[p]):
            in2_ref[q, :, here] = out2_ref[q, :, here]

    def take_in(p):
        @pl.loop(1, GROUPS)
        def _(i):
            hop2(p, i).wait_recv()

        for q in range(*CHUNKS[p]):
            for c in range(WORDS // 128):
                flipped = in2_ref[q, c].T
                got_ref[q, c * 128 : c * 128 + 128] = flipped
                if c == 2:
                    last_ref[pl.ds(q, CAP, stride=OCTANTS), :] = flipped[
                        ENTRY_ROWS - 256 : ENTRY_ROWS - 256 + CAP
                    ]

    part_ref[...] = jnp.zeros(part_ref.shape, jnp.float32)
    wide_ref[...] = jnp.zeros(wide_ref.shape, jnp.bfloat16)
    acc_ref[...] = jnp.zeros(acc_ref.shape, jnp.float32)
    for copy in small[:5]:
        copy.wait()
    build_table(euler_ref, angle_ref, table_ref)
    find_slots(owner_ref, element_ref, active_ref, owned_ref, rank_ref, single_ref, label_ref)

    def spread(block, buffer, u, q):
        parts = [part_ref[buffer, u, n] for n in range(9)]
        single = parts[8]
        for shift in (4, 2, 1):
            single = single + pltpu.roll(single, shift, 0)
        main_halves = halves(sum_sublanes(parts[:8], row))
        single_halves = halves(single)
        for n in range(2):
            lanes = slice(u * 256 + n * 128, u * 256 + n * 128 + 128)
            for pair in range(CAP // 2):
                rows = slice(16 * pair, 16 * pair + 16)
                wide_ref[rows, lanes] = rank_ref[block, rows] * main_halves[n]
            for part in range(3):
                rows = slice(16 * part, 16 * part + 16)
                target = slice(ENTRY_ROWS + 16 * part, ENTRY_ROWS + 16 * part + 16)
                wide_ref[target, lanes] = single_ref[block, rows] * single_halves[n]
        if isinstance(q, int) and q >= 3:
            return
        rows = pl.ds(pl.multiple_of(16 * q, 16), 16)
        wide_ref[LABEL_ROWS:, u * 256 : u * 256 + 128] = label_ref[block, rows]

    def place(step):
        acc_ref[...] += lax.dot_general(
            owned_ref[step], wide_ref[...], NT_DIMS, preferred_element_type=jnp.float32
        )

    def finish(q):
        for c in range(WORDS // 128):
            out1_ref[q, c] = acc_ref[:, c * 128 : c * 128 + 128]
        acc_ref[...] = jnp.zeros(acc_ref.shape, jnp.float32)

    todo = {q: [] for q in range(OCTANTS + 1)}
    for p, (_, stop) in enumerate(CHUNKS):
        todo[stop].append((start1, p))
        todo[min(stop + 1, OCTANTS)].append((pass_on, p))
        todo[min(stop + 3, OCTANTS)].append((take_in, p))
    arrived = 0

    for q in range(OCTANTS):
        first = (q * per_octant) // 8
        stop = -(-((q + 1) * per_octant) // 8)
        fresh = first if first * 8 == q * per_octant else first + 1
        while id_cuts[arrived] < stop * 8:
            ids_copy(arrived).wait()
            arrived += 1

        @pl.loop(0, steps)
        def _(step, q=q, fresh=fresh, stop=stop):
            buffer = step & 1
            before = lax.rem(step + steps - 1, steps)
            label_octant = jnp.where(step == 0, max(q - 1, 0), min(q, 2)) if q < 4 else q
            for u in range(UNROLL):
                spread(before * UNROLL + u, 1 - buffer, u, label_octant)
                if u == UNROLL - 1:
                    place(before)
                block = step * UNROLL + u
                columns = pl.ds(pl.multiple_of(block * 128, 128), 128)
                sums = None if q == 0 else [carry_ref[block, n] for n in range(9)]
                for t in range(fresh, stop):
                    terms = rotation_terms(
                        *lookup(table_ref, ids_ref[8 * t : 8 * t + 8, columns])
                    )
                    split = (q + 1) * per_octant - 8 * t
                    if split < 8:
                        inside = row < split
                        for n in range(9):
                            carry_ref[block, n] = jnp.where(inside, 0.0, terms[n])
                        terms = [jnp.where(inside, v, 0.0) for v in terms]
                    sums = terms if sums is None else [s + v for s, v in zip(sums, terms)]
                for n, entry in enumerate(octant_entries(sums, per_octant)):
                    part_ref[buffer, u, n] = entry

            @pl.when(step == 0)
            def _():
                if q > 0:
                    finish(q - 1)
                else:
                    acc_ref[...] = jnp.zeros(acc_ref.shape, jnp.float32)
                for action, p in todo[q]:
                    action(p)

    for u in range(UNROLL):
        spread((steps - 1) * UNROLL + u, 1, u, OCTANTS - 1)
    place(steps - 1)
    finish(OCTANTS - 1)
    rest = sorted(todo[OCTANTS], key=lambda item: ORDER[item[0].__name__] + item[1])
    for action, p in rest[:1]:
        action(p)
    for copy in small[5:]:
        copy.wait()
    layer_copy().wait()
    above_ref[...] = jnp.where(fe == MEMBERS - 1, 0.0, land_ref[...])
    for n, trial in enumerate(trial_stress(below_ref, above_ref, stress_ref, grads_ref)):
        trial_ref[n] = trial
    for action, p in rest[1:]:
        action(p)

    label_value = lax.broadcasted_iota(jnp.int32, (NODES, 128), 0).astype(jnp.float32) + 1.0
    ones = jnp.ones((16, 128), jnp.bfloat16)
    sums = jnp.zeros((160, NODES), jnp.float32)
    for r in range(0, CAP, 2):
        left, right = [], []
        for n in (r, r + 1):
            values = jnp.concatenate(
                [got_ref[q, 8 * n : 8 * n + 8] for q in range(OCTANTS)]
                + [last_ref[8 * n : 8 * n + 8]],
                axis=0,
            )
            high = values.astype(jnp.bfloat16).astype(jnp.float32)
            both = jnp.concatenate([high, values - high], axis=0).astype(jnp.bfloat16)
            left.append(jnp.concatenate([both, ones], axis=0))
            line = LABEL_ROWS + n % 16
            hit = label_value == got_ref[n // 16, line : line + 1, :]
            right.append(hit.astype(jnp.bfloat16))
        sums = sums + lax.dot_general(
            jnp.concatenate(left, axis=1),
            jnp.concatenate(right, axis=1),
            NT_DIMS,
            preferred_element_type=jnp.float32,
        )
    for half in range(2):
        lanes = slice(half * 128, half * 128 + 128)
        sums_ref[half, :72] = sums[:72, lanes] + sums[72:144, lanes]
        sums_ref[half, 72:80] = sums[144:152, lanes]
    trial = [trial_ref[n] for n in range(6)]
    updated = stress_update(sums_ref, trial, resistance_ref)
    placed = nodal_parts(updated, weights_ref, gather_ref)
    for comp in range(3):
        top_ref[comp] = layer_forces(placed, comp, 1)
    top_copy().start()
    for component in range(6):
        stress_out[component] = updated[component]
    owned = [layer_forces(placed, comp, 0) for comp in range(3)]
    for p in range(len(CHUNKS)):

        @pl.loop(1, MEMBERS)
        def _(i, p=p):
            hop1(p, i).wait_send()

        @pl.loop(1, GROUPS)
        def _(i, p=p):
            hop2(p, i).wait_send()

    top_copy().wait()
    for comp in range(3):
        forces_out[comp] = owned[comp] + jnp.where(fe == 0, 0.0, under_ref[comp])


ORDER = {"start1": 0, "pass_on": 10, "take_in": 20}


def fused_step(
    grain_ids, euler_angles, owner, element, active, below, stress_old, resistance, quad_weights
):
    grads, forces = gradient_matrices()
    bricks = grain_ids.shape[1]
    blocks = bricks // 128
    hop = pltpu.VMEM((OCTANTS, WORDS // 128, DEVICES, 128), jnp.float32)
    vmem = pl.BlockSpec(memory_space=pltpu.VMEM)
    line = pltpu.VMEM((1, bricks), jnp.int32)
    layer = pltpu.VMEM(below.shape, jnp.float32)
    chunks = len(CHUNKS)
    return pl.pallas_call(
        exchange_kernel,
        out_shape=(
            jax.ShapeDtypeStruct(stress_old.shape, jnp.float32),
            jax.ShapeDtypeStruct(below.shape, jnp.float32),
        ),
        in_specs=[pl.BlockSpec(memory_space=pltpu.HBM)] * 11,
        out_specs=(vmem, vmem),
        scratch_shapes=[
            pltpu.VMEM(grain_ids.shape, jnp.int32),
            pltpu.VMEM(euler_angles.shape, jnp.float32),
            line,
            line,
            line,
            pltpu.VMEM(below.shape, jnp.float32),
            pltpu.VMEM((3, 32, 128), jnp.float32),
            pltpu.VMEM((64, 8, 128), jnp.int32),
            pltpu.VMEM((blocks, 9, 8, 128), jnp.float32),
            pltpu.VMEM((blocks // UNROLL, DEVICES, 256 * UNROLL), jnp.bfloat16),
            pltpu.VMEM((blocks, ENTRY_ROWS, 128), jnp.bfloat16),
            pltpu.VMEM((blocks, 48, 128), jnp.bfloat16),
            pltpu.VMEM((blocks, 48, 128), jnp.bfloat16),
            pltpu.VMEM((2, UNROLL, 9, 8, 128), jnp.float32),
            pltpu.VMEM((WORDS, 256 * UNROLL), jnp.bfloat16),
            pltpu.VMEM((DEVICES, WORDS), jnp.float32),
            hop,
            hop,
            hop,
            hop,
            pltpu.VMEM((OCTANTS, WORDS, 128), jnp.float32),
            pltpu.VMEM((OCTANTS * CAP, 128), jnp.float32),
            pltpu.VMEM((2, 80, 128), jnp.float32),
            pltpu.VMEM(stress_old.shape, jnp.float32),
            pltpu.VMEM(resistance.shape, jnp.float32),
            pltpu.VMEM(quad_weights.shape, jnp.int32),
            pltpu.VMEM(grads.shape, jnp.float32),
            pltpu.VMEM(forces.shape, jnp.float32),
            layer,
            layer,
            layer,
            layer,
            pltpu.VMEM(stress_old.shape, jnp.float32),
            pltpu.SemaphoreType.DMA((5,)),
            pltpu.SemaphoreType.DMA((10,)),
            pltpu.SemaphoreType.DMA((chunks, MEMBERS)),
            pltpu.SemaphoreType.DMA((chunks, MEMBERS)),
            pltpu.SemaphoreType.DMA((chunks, GROUPS)),
            pltpu.SemaphoreType.DMA((chunks, GROUPS)),
            pltpu.SemaphoreType.DMA((4,)),
        ],
        compiler_params=pltpu.CompilerParams(
            vmem_limit_bytes=EXCHANGE_VMEM, collective_id=0, has_side_effects=True
        ),
        name="fused_step",
    )(
        grain_ids,
        euler_angles,
        owner.reshape(1, bricks),
        element.reshape(1, bricks),
        active.reshape(1, bricks),
        below,
        stress_old,
        resistance,
        quad_weights,
        jnp.asarray(grads),
        jnp.asarray(forces),
    )


def body(
    grain_ids,
    euler_angles,
    brick_active,
    brick_owner,
    brick_element,
    displacement,
    stress_old,
    resistance,
    quad_weights,
):
    return fused_step(
        grain_ids,
        euler_angles,
        brick_owner,
        brick_element,
        brick_active,
        displacement,
        stress_old,
        resistance,
        quad_weights,
    )


def solution(mesh):
    placed = (
        P(None, ("ca", "fe")),
        P(),
        P(("ca", "fe")),
        P(("ca", "fe"), None),
        P(("ca", "fe")),
        P(None, ("ca", "fe"), None),
        P(None, None, ("ca", "fe")),
        P(None, None, ("ca", "fe")),
        P(None, ("ca", "fe")),
    )
    return jax.shard_map(
        body,
        mesh=mesh,
        in_specs=placed,
        out_specs=(P(None, None, ("ca", "fe")), P(None, ("ca", "fe"), None)),
        check_vma=False,
    )
```

time: 91.5 us -> 73.9 us (0.81)
  the two profiles are of different devices: /device:TPU:32 before, /device:TPU:1 now
where the time goes in v3:
time: 73.9 us; the launch traced here: 73.7 us
  Pallas kernels  70.4 us (95%)
  local copies, waits for them, and re-layouts  2.67 us (4%)
    pallas_call x1, Pallas kernels, fused_step(): pl.pallas_call(exchange_kernel, out_shape=(jax.ShapeDtypeStruct(stress_ol...  70.4 us
    unnamed x2, local copies, waits for them, and re-layouts  2.67 us

profile of v3, /device:TPU:1, one launch (start us, length us, event | category | flops | bytes accessed | tf_op | source)
XLA Modules:
  0.0 73.7 jit_solution(12623221969916204574)
XLA Ops:
  0.6 70.4 %fused_step.1 = (f32[6,8,225]{2,1,0:T(8,128)}, f32[3,1,256]{2,1,0:T(1,128)}) custom-call(s32[216,2048]{1,0:T(8,128)} %ids_hbm.1, f32[3,4096]{1,0:T(4,128)} %euler_hbm.1, s32[1,2048]{1,0:T(1,128)} %bitcast.3, s32[1,2048]{1,0:T(1,128)} %bitcast.4, s32[1,2048]{1,0:T(1,128)} %bitcast.5, f32[3,1,256]{2,1,0:T(1,128)} %below_hbm.1, f32[6,8,225]{2,1,0:T(8,128)} %stress_hbm.1, ...), custom_call_target="tpu_custom_call" | custom-call | tf_op jit(solution)/shard_map/fused_step/pallas_call | solution.py:768
  71.0 1.4 %copy.15 = f32[6,8,225]{2,1,0:T(8,128)} copy(f32[6,8,225]{2,1,0:T(8,128)} %get-tuple-element.4) | data formatting | bytes 86400
  72.4 1.3 %copy.16 = f32[3,1,256]{2,1,0:T(1,128)} copy(f32[3,1,256]{2,1,0:T(1,128)} %get-tuple-element.5) | data formatting | bytes 6144

commit v4 on v3

--- a/solution.py
+++ b/solution.py
@@ -157,36 +157,10 @@
     ]
 
 
-def swapped(values, step, keep):
-    return jnp.where(keep, pltpu.roll(values, 8 - step, 0), pltpu.roll(values, step, 0))
-
-
-def sum_sublanes(parts, row):
-    half = len(parts) // 2
-    low4 = row < 4
-    level = [
-        jnp.where(low4, parts[n], parts[n + half])
-        + pltpu.roll(jnp.where(low4, parts[n + half], parts[n]), 4, 0)
-        for n in range(half)
-    ]
-    for step in (2, 1):
-        keep = (row & step) == 0
-        if len(level) == 1:
-            level = [level[0] + swapped(level[0], step, keep)]
-            continue
-        half = len(level) // 2
-        level = [
-            jnp.where(keep, level[n], level[n + half])
-            + swapped(jnp.where(keep, level[n + half], level[n]), step, keep)
-            for n in range(half)
-        ]
-    return level[0]
-
-
 NT_DIMS = (((1,), (1,)), ((), ()))
 MESH = pl.DeviceIdType.MESH
 OCTANTS = 8
-CHUNKS = ((0, 2), (2, 4), (4, 6), (6, 7), (7, 8))
+CHUNKS = ((0, 2), (2, 4), (4, 5), (5, 6), (6, 7), (7, 8))
 UNROLL = 4
 WORDS = 384
 ENTRY_ROWS = 8 * CAP
@@ -422,6 +396,8 @@
     single_ref,
     label_ref,
     part_ref,
+    pool_ref,
+    stage_ref,
     wide_ref,
     acc_ref,
     out1_ref,
@@ -430,6 +406,7 @@
     in2_ref,
     got_ref,
     last_ref,
+    hit_ref,
     sums_ref,
     stress_ref,
     resistance_ref,
@@ -595,7 +572,11 @@
                         ENTRY_ROWS - 256 : ENTRY_ROWS - 256 + CAP
                     ]
 
-    part_ref[...] = jnp.zeros(part_ref.shape, jnp.float32)
+    part_ref[...] = jnp.zeros(part_ref.shape, jnp.bfloat16)
+    target = jnp.minimum(lax.broadcasted_iota(jnp.int32, (16, 160), 0), 8)
+    source = lax.broadcasted_iota(jnp.int32, (16, 160), 1)
+    source = jnp.right_shift(jnp.where(source >= 80, source - 80, source), 3)
+    pool_ref[...] = jnp.where(target == source, 1.0, 0.0).astype(jnp.bfloat16)
     wide_ref[...] = jnp.zeros(wide_ref.shape, jnp.bfloat16)
     acc_ref[...] = jnp.zeros(acc_ref.shape, jnp.float32)
     for copy in small[:5]:
@@ -603,13 +584,20 @@
     build_table(euler_ref, angle_ref, table_ref)
     find_slots(owner_ref, element_ref, active_ref, owned_ref, rank_ref, single_ref, label_ref)
 
-    def spread(block, buffer, u, q):
-        parts = [part_ref[buffer, u, n] for n in range(9)]
-        single = parts[8]
-        for shift in (4, 2, 1):
-            single = single + pltpu.roll(single, shift, 0)
-        main_halves = halves(sum_sublanes(parts[:8], row))
-        single_halves = halves(single)
+    def keep_parts(u, entries):
+        stacked = jnp.concatenate(entries + [jnp.zeros((8, 128), jnp.float32)], axis=0)
+        high = stacked.astype(jnp.bfloat16)
+        lanes = slice(u * 128, u * 128 + 128)
+        part_ref[:80, lanes] = high
+        part_ref[80:, lanes] = (stacked - high.astype(jnp.float32)).astype(jnp.bfloat16)
+
+    def totals():
+        return jnp.dot(pool_ref[...], part_ref[...], preferred_element_type=jnp.float32)
+
+    def spread(block, u, q, total):
+        columns = slice(u * 128, u * 128 + 128)
+        main_halves = halves(total[:8, columns])
+        single_halves = halves(total[8:, columns])
         for n in range(2):
             lanes = slice(u * 256 + n * 128, u * 256 + n * 128 + 128)
             for pair in range(CAP // 2):
@@ -634,11 +622,14 @@
             out1_ref[q, c] = acc_ref[:, c * 128 : c * 128 + 128]
         acc_ref[...] = jnp.zeros(acc_ref.shape, jnp.float32)
 
-    todo = {q: [] for q in range(OCTANTS + 1)}
-    for p, (_, stop) in enumerate(CHUNKS):
-        todo[stop].append((start1, p))
-        todo[min(stop + 1, OCTANTS)].append((pass_on, p))
-        todo[min(stop + 3, OCTANTS)].append((take_in, p))
+    todo = {}
+    for action, times in (
+        (start1, ((2, 0), (4, 0), (5, 0), (6, 0), (7, 0), (8, 0))),
+        (pass_on, ((3, 1), (5, 1), (6, 0), (7, 0), (7, 3), (8, 0))),
+        (take_in, ((4, 3), (6, 3), (7, 3), (8, 0), (8, 0), (8, 0))),
+    ):
+        for p, time in enumerate(times):
+            todo.setdefault(time, []).append((action, p))
     arrived = 0
 
     for q in range(OCTANTS):
@@ -651,16 +642,19 @@
 
         @pl.loop(0, steps)
         def _(step, q=q, fresh=fresh, stop=stop):
-            buffer = step & 1
             before = lax.rem(step + steps - 1, steps)
             label_octant = jnp.where(step == 0, max(q - 1, 0), min(q, 2)) if q < 4 else q
+            if q > 0:
+                for u in range(UNROLL):
+                    stage_ref[0, u] = carry_ref[step * UNROLL + u]
+            total = totals()
             for u in range(UNROLL):
-                spread(before * UNROLL + u, 1 - buffer, u, label_octant)
+                spread(before * UNROLL + u, u, label_octant, total)
                 if u == UNROLL - 1:
                     place(before)
                 block = step * UNROLL + u
                 columns = pl.ds(pl.multiple_of(block * 128, 128), 128)
-                sums = None if q == 0 else [carry_ref[block, n] for n in range(9)]
+                sums = None if q == 0 else [stage_ref[0, u, n] for n in range(9)]
                 for t in range(fresh, stop):
                     terms = rotation_terms(
                         *lookup(table_ref, ids_ref[8 * t : 8 * t + 8, columns])
@@ -669,11 +663,14 @@
                     if split < 8:
                         inside = row < split
                         for n in range(9):
-                            carry_ref[block, n] = jnp.where(inside, 0.0, terms[n])
+                            stage_ref[1, u, n] = jnp.where(inside, 0.0, terms[n])
                         terms = [jnp.where(inside, v, 0.0) for v in terms]
                     sums = terms if sums is None else [s + v for s, v in zip(sums, terms)]
-                for n, entry in enumerate(octant_entries(sums, per_octant)):
-                    part_ref[buffer, u, n] = entry
+                keep_parts(u, octant_entries(sums, per_octant))
+
+            if q < OCTANTS - 1:
+                for u in range(UNROLL):
+                    carry_ref[step * UNROLL + u] = stage_ref[1, u]
 
             @pl.when(step == 0)
             def _():
@@ -681,14 +678,21 @@
                     finish(q - 1)
                 else:
                     acc_ref[...] = jnp.zeros(acc_ref.shape, jnp.float32)
-                for action, p in todo[q]:
-                    action(p)
-
+
+            for late in range(4):
+                if (q, late) in todo:
+
+                    @pl.when(step == late * steps // 4)
+                    def _(late=late):
+                        for action, p in todo[q, late]:
+                            action(p)
+
+    total = totals()
     for u in range(UNROLL):
-        spread((steps - 1) * UNROLL + u, 1, u, OCTANTS - 1)
+        spread((steps - 1) * UNROLL + u, u, OCTANTS - 1, total)
     place(steps - 1)
     finish(OCTANTS - 1)
-    rest = sorted(todo[OCTANTS], key=lambda item: ORDER[item[0].__name__] + item[1])
+    rest = sorted(todo[OCTANTS, 0], key=lambda item: ORDER[item[0].__name__] + item[1])
     for action, p in rest[:1]:
         action(p)
     for copy in small[5:]:
@@ -697,36 +701,46 @@
     above_ref[...] = jnp.where(fe == MEMBERS - 1, 0.0, land_ref[...])
     for n, trial in enumerate(trial_stress(below_ref, above_ref, stress_ref, grads_ref)):
         trial_ref[n] = trial
-    for action, p in rest[1:]:
+    for action, p in rest[1:-1]:
         action(p)
 
+    ones = jnp.ones((16, 128), jnp.bfloat16)
+
+    def owner_sums(octants, last, rows):
+        sums = jnp.zeros((rows, NODES), jnp.float32)
+        for r in range(0, CAP, 2):
+            left = []
+            for n in (r, r + 1):
+                values = [got_ref[q, 8 * n : 8 * n + 8] for q in octants]
+                if last:
+                    values.append(last_ref[8 * n : 8 * n + 8])
+                values = jnp.concatenate(values, axis=0)
+                high = values.astype(jnp.bfloat16).astype(jnp.float32)
+                both = jnp.concatenate([high, values - high], axis=0).astype(jnp.bfloat16)
+                left.append(both if last else jnp.concatenate([both, ones], axis=0))
+            sums = sums + lax.dot_general(
+                jnp.concatenate(left, axis=1),
+                hit_ref[r // 2],
+                NT_DIMS,
+                preferred_element_type=jnp.float32,
+            )
+        return sums
+
     label_value = lax.broadcasted_iota(jnp.int32, (NODES, 128), 0).astype(jnp.float32) + 1.0
-    ones = jnp.ones((16, 128), jnp.bfloat16)
-    sums = jnp.zeros((160, NODES), jnp.float32)
-    for r in range(0, CAP, 2):
-        left, right = [], []
-        for n in (r, r + 1):
-            values = jnp.concatenate(
-                [got_ref[q, 8 * n : 8 * n + 8] for q in range(OCTANTS)]
-                + [last_ref[8 * n : 8 * n + 8]],
-                axis=0,
-            )
-            high = values.astype(jnp.bfloat16).astype(jnp.float32)
-            both = jnp.concatenate([high, values - high], axis=0).astype(jnp.bfloat16)
-            left.append(jnp.concatenate([both, ones], axis=0))
-            line = LABEL_ROWS + n % 16
-            hit = label_value == got_ref[n // 16, line : line + 1, :]
-            right.append(hit.astype(jnp.bfloat16))
-        sums = sums + lax.dot_general(
-            jnp.concatenate(left, axis=1),
-            jnp.concatenate(right, axis=1),
-            NT_DIMS,
-            preferred_element_type=jnp.float32,
-        )
+    for n in range(CAP):
+        line = LABEL_ROWS + n % 16
+        hit = label_value == got_ref[n // 16, line : line + 1, :]
+        lanes = slice((n & 1) * 128, (n & 1) * 128 + 128)
+        hit_ref[n // 2, :, lanes] = hit.astype(jnp.bfloat16)
+    early = owner_sums(range(OCTANTS - 1), False, 128)
+    action, p = rest[-1]
+    action(p)
+    late = owner_sums([OCTANTS - 1], True, 32)
     for half in range(2):
         lanes = slice(half * 128, half * 128 + 128)
-        sums_ref[half, :72] = sums[:72, lanes] + sums[72:144, lanes]
-        sums_ref[half, 72:80] = sums[144:152, lanes]
+        sums_ref[half, :56] = early[:56, lanes] + early[56:112, lanes]
+        sums_ref[half, 56:72] = late[:16, lanes] + late[16:32, lanes]
+        sums_ref[half, 72:80] = early[112:120, lanes]
     trial = [trial_ref[n] for n in range(6)]
     updated = stress_update(sums_ref, trial, resistance_ref)
     placed = nodal_parts(updated, weights_ref, gather_ref)
@@ -787,6 +801,8 @@
             pltpu.VMEM((blocks, ENTRY_ROWS, 128), jnp.bfloat16),
             pltpu.VMEM((blocks, 48, 128), jnp.bfloat16),
             pltpu.VMEM((blocks, 48, 128), jnp.bfloat16),
+            pltpu.VMEM((160, 128 * UNROLL), jnp.bfloat16),
+            pltpu.VMEM((16, 160), jnp.bfloat16),
             pltpu.VMEM((2, UNROLL, 9, 8, 128), jnp.float32),
             pltpu.VMEM((WORDS, 256 * UNROLL), jnp.bfloat16),
             pltpu.VMEM((DEVICES, WORDS), jnp.float32),
@@ -796,6 +812,7 @@
             hop,
             pltpu.VMEM((OCTANTS, WORDS, 128), jnp.float32),
             pltpu.VMEM((OCTANTS * CAP, 128), jnp.float32),
+            pltpu.VMEM((CAP // 2, NODES, 256), jnp.bfloat16),
             pltpu.VMEM((2, 80, 128), jnp.float32),
             pltpu.VMEM(stress_old.shape, jnp.float32),
             pltpu.VMEM(resistance.shape, jnp.float32),
@@ -834,6 +851,29 @@
     )
 
 
+def handing_kernel(stress_in, forces_in, stress_out, forces_out, sem):
+    copies = [
+        pltpu.make_async_copy(stress_in, stress_out, sem.at[0]),
+        pltpu.make_async_copy(forces_in, forces_out, sem.at[1]),
+    ]
+    for copy in copies:
+        copy.start()
+    for copy in copies:
+        copy.wait()
+
+
+def handed_out(stress, forces):
+    hbm = pl.BlockSpec(memory_space=pltpu.HBM)
+    return pl.pallas_call(
+        handing_kernel,
+        out_shape=tuple(jax.ShapeDtypeStruct(x.shape, x.dtype) for x in (stress, forces)),
+        in_specs=[hbm, hbm],
+        out_specs=(hbm, hbm),
+        scratch_shapes=[pltpu.SemaphoreType.DMA((2,))],
+        name="handed_out",
+    )(stress, forces)
+
+
 def body(
     grain_ids,
     euler_angles,
@@ -845,16 +885,18 @@
     resistance,
     quad_weights,
 ):
-    return fused_step(
-        grain_ids,
-        euler_angles,
-        brick_owner,
-        brick_element,
-        brick_active,
-        displacement,
-        stress_old,
-        resistance,
-        quad_weights,
+    return handed_out(
+        *fused_step(
+            grain_ids,
+            euler_angles,
+            brick_owner,
+            brick_element,
+            brick_active,
+            displacement,
+            stress_old,
+            resistance,
+            quad_weights,
+        )
     )
 
 

time: 73.9 us -> 72.6 us (0.982)
  local copies, waits for them, and re-layouts: 2.67 us -> 0 us
  Pallas kernels: 70.4 us -> 71.9 us
    pallas_call x0 -> x1, Pallas kernels: none -> 2.7 us  [handed_out(): pl.pallas_call(handing_kernel, out_shape=tuple((jax.ShapeDtypeStruct(x.sh...]
    unnamed x2 -> x0, local copies, waits for them, and re-layouts: 2.67 us -> none
    pallas_call x1, Pallas kernels: 70.4 us -> 69.2 us  [fused_step(): pl.pallas_call(exchange_kernel, out_shape=(jax.ShapeDtypeStruct(stress_ol...]
where the time goes in v4:
time: 72.6 us; the launch traced here: 72.5 us
  Pallas kernels  71.9 us (99%)
    pallas_call x1, Pallas kernels, fused_step(): pl.pallas_call(exchange_kernel, out_shape=(jax.ShapeDtypeStruct(stress_ol...  69.2 us
    pallas_call x1, Pallas kernels, handed_out(): pl.pallas_call(handing_kernel, out_shape=tuple((jax.ShapeDtypeStruct(x.sh...  2.7 us

profile of v4, /device:TPU:1, one launch (start us, length us, event | category | flops | bytes accessed | tf_op | source)
XLA Modules:
  0.0 72.5 jit_solution(2572834892999479158)
XLA Ops:
  0.6 69.2 %fused_step.1 = (f32[6,8,225]{2,1,0:T(8,128)}, f32[3,1,256]{2,1,0:T(1,128)}) custom-call(s32[216,2048]{1,0:T(8,128)} %ids_hbm.1, f32[3,4096]{1,0:T(4,128)} %euler_hbm.1, s32[1,2048]{1,0:T(1,128)} %bitcast.3, s32[1,2048]{1,0:T(1,128)} %bitcast.4, s32[1,2048]{1,0:T(1,128)} %bitcast.5, f32[3,1,256]{2,1,0:T(1,128)} %below_hbm.1, f32[6,8,225]{2,1,0:T(8,128)} %stress_hbm.1, ...), custom_call_target="tpu_custom_call" | custom-call | tf_op jit(solution)/shard_map/fused_step/pallas_call | solution.py:782
  69.8 2.7 %handed_out.1 = (f32[6,8,225]{2,1,0:T(8,128)}, f32[3,1,256]{2,1,0:T(1,128)}) custom-call(f32[6,8,225]{2,1,0:T(8,128)} %get-tuple-element.4.stress_in, f32[3,1,256]{2,1,0:T(1,128)} %get-tuple-element.5.forces_in), custom_call_target="tpu_custom_call" | custom-call | tf_op jit(solution)/shard_map/handed_out/pallas_call | solution.py:867

commit v5 on v4

--- a/solution.py
+++ b/solution.py
@@ -1,3 +1,4 @@
+import collections
 import functools
 import math
 
@@ -116,13 +117,15 @@
         table_ref[32 + row] = jnp.broadcast_to(word_b[row : row + 1], (8, 128))
 
 
-def lookup(table_ref, ids):
+def lookup(table_ref, ids, work):
     lanes = ids & 127
     bits = [(ids & (128 << level)) != 0 for level in range(5)]
     words = ([], [])
     for row in range(32):
         for n, stack in enumerate(words):
             merge_tree(stack, lane_pick(table_ref[n * 32 + row], lanes), row, bits)
+        if work and row % 3 == 2:
+            work.popleft()()
     return words[0][0], words[1][0]
 
 
@@ -486,8 +489,8 @@
         return pltpu.make_async_remote_copy(
             src_ref=out1_ref.at[octants, :, there],
             dst_ref=in1_ref.at[octants, :, here],
-            send_sem=send1_sem.at[p, i],
-            recv_sem=recv1_sem.at[p, i],
+            send_sem=send1_sem.at[p],
+            recv_sem=recv1_sem.at[p],
             device_id=(ca, member(i)),
             device_id_type=MESH,
         )
@@ -499,9 +502,33 @@
         return pltpu.make_async_remote_copy(
             src_ref=out2_ref.at[octants, :, there],
             dst_ref=in2_ref.at[octants, :, here],
-            send_sem=send2_sem.at[p, i],
-            recv_sem=recv2_sem.at[p, i],
+            send_sem=send2_sem.at[p],
+            recv_sem=recv2_sem.at[p],
             device_id=(group(i), fe),
+            device_id_type=MESH,
+        )
+
+    def all1(p):
+        octants = pl.ds(CHUNKS[p][0], CHUNKS[p][1] - CHUNKS[p][0])
+        rows = pl.ds(0, DEVICES - GROUPS)
+        return pltpu.make_async_remote_copy(
+            src_ref=out1_ref.at[octants, :, rows],
+            dst_ref=in1_ref.at[octants, :, rows],
+            send_sem=send1_sem.at[p],
+            recv_sem=recv1_sem.at[p],
+            device_id=(ca, member(1)),
+            device_id_type=MESH,
+        )
+
+    def all2(p):
+        octants = pl.ds(CHUNKS[p][0], CHUNKS[p][1] - CHUNKS[p][0])
+        rows = pl.ds(0, DEVICES - MEMBERS)
+        return pltpu.make_async_remote_copy(
+            src_ref=out2_ref.at[octants, :, rows],
+            dst_ref=in2_ref.at[octants, :, rows],
+            send_sem=send2_sem.at[p],
+            recv_sem=recv2_sem.at[p],
+            device_id=(group(1), fe),
             device_id_type=MESH,
         )
 
@@ -530,8 +557,7 @@
             pl.semaphore_wait(barrier, MEMBERS + GROUPS - 2)
             layer_copy().start()
 
-        @pl.loop(1, MEMBERS)
-        def _(i):
+        for i in range(1, MEMBERS):
             hop1(p, i).start()
 
         here = pl.ds(pl.multiple_of(fe * GROUPS, 8), GROUPS)
@@ -539,9 +565,7 @@
             in1_ref[q, :, here] = out1_ref[q, :, here]
 
     def pass_on(p):
-        @pl.loop(1, MEMBERS)
-        def _(i):
-            hop1(p, i).wait_recv()
+        all1(p).wait_recv()
 
         for q in range(*CHUNKS[p]):
             for c in range(WORDS // 128):
@@ -550,8 +574,7 @@
                         q, c, pl.ds(g, MEMBERS, stride=GROUPS), :
                     ]
 
-        @pl.loop(1, GROUPS)
-        def _(i):
+        for i in range(1, GROUPS):
             hop2(p, i).start()
 
         here = pl.ds(pl.multiple_of(ca * MEMBERS, 8), MEMBERS)
@@ -559,9 +582,7 @@
             in2_ref[q, :, here] = out2_ref[q, :, here]
 
     def take_in(p):
-        @pl.loop(1, GROUPS)
-        def _(i):
-            hop2(p, i).wait_recv()
+        all2(p).wait_recv()
 
         for q in range(*CHUNKS[p]):
             for c in range(WORDS // 128):
@@ -591,26 +612,38 @@
         part_ref[:80, lanes] = high
         part_ref[80:, lanes] = (stacked - high.astype(jnp.float32)).astype(jnp.bfloat16)
 
-    def totals():
-        return jnp.dot(pool_ref[...], part_ref[...], preferred_element_type=jnp.float32)
+    def totals(out):
+        out["sum"] = jnp.dot(pool_ref[...], part_ref[...], preferred_element_type=jnp.float32)
 
     def spread(block, u, q, total):
-        columns = slice(u * 128, u * 128 + 128)
-        main_halves = halves(total[:8, columns])
-        single_halves = halves(total[8:, columns])
-        for n in range(2):
+        parts = {}
+
+        def split():
+            columns = slice(u * 128, u * 128 + 128)
+            parts["main"] = halves(total["sum"][:8, columns])
+            parts["single"] = halves(total["sum"][8:, columns])
+
+        def main(n, first):
             lanes = slice(u * 256 + n * 128, u * 256 + n * 128 + 128)
-            for pair in range(CAP // 2):
+            for pair in range(first, first + 5):
                 rows = slice(16 * pair, 16 * pair + 16)
-                wide_ref[rows, lanes] = rank_ref[block, rows] * main_halves[n]
+                wide_ref[rows, lanes] = rank_ref[block, rows] * parts["main"][n]
+
+        def single(n):
+            lanes = slice(u * 256 + n * 128, u * 256 + n * 128 + 128)
             for part in range(3):
                 rows = slice(16 * part, 16 * part + 16)
                 target = slice(ENTRY_ROWS + 16 * part, ENTRY_ROWS + 16 * part + 16)
-                wide_ref[target, lanes] = single_ref[block, rows] * single_halves[n]
-        if isinstance(q, int) and q >= 3:
-            return
-        rows = pl.ds(pl.multiple_of(16 * q, 16), 16)
-        wide_ref[LABEL_ROWS:, u * 256 : u * 256 + 128] = label_ref[block, rows]
+                wide_ref[target, lanes] = single_ref[block, rows] * parts["single"][n]
+            if n == 0 and not (isinstance(q, int) and q >= 3):
+                rows = pl.ds(pl.multiple_of(16 * q, 16), 16)
+                wide_ref[LABEL_ROWS:, u * 256 : u * 256 + 128] = label_ref[block, rows]
+
+        yield split
+        for n in range(2):
+            for first in range(0, CAP // 2, 5):
+                yield functools.partial(main, n, first)
+            yield functools.partial(single, n)
 
     def place(step):
         acc_ref[...] += lax.dot_general(
@@ -647,26 +680,38 @@
             if q > 0:
                 for u in range(UNROLL):
                     stage_ref[0, u] = carry_ref[step * UNROLL + u]
-            total = totals()
+            total = {}
+            work = collections.deque()
+            totals(total)
             for u in range(UNROLL):
-                spread(before * UNROLL + u, u, label_octant, total)
-                if u == UNROLL - 1:
-                    place(before)
-                block = step * UNROLL + u
-                columns = pl.ds(pl.multiple_of(block * 128, 128), 128)
-                sums = None if q == 0 else [stage_ref[0, u, n] for n in range(9)]
+                work.extend(spread(before * UNROLL + u, u, label_octant, total))
+            work.append(functools.partial(place, before))
+            state = {}
+
+            def decode(u, t, words):
+                terms = rotation_terms(*words)
+                split = (q + 1) * per_octant - 8 * t
+                if split < 8:
+                    inside = row < split
+                    for n in range(9):
+                        stage_ref[1, u, n] = jnp.where(inside, 0.0, terms[n])
+                    terms = [jnp.where(inside, v, 0.0) for v in terms]
+                if t == fresh:
+                    if q > 0:
+                        terms = [stage_ref[0, u, n] + v for n, v in enumerate(terms)]
+                else:
+                    terms = [s + v for s, v in zip(state[u], terms)]
+                state[u] = terms
+                if t == stop - 1:
+                    keep_parts(u, octant_entries(terms, per_octant))
+
+            for u in range(UNROLL):
+                columns = pl.ds(pl.multiple_of((step * UNROLL + u) * 128, 128), 128)
                 for t in range(fresh, stop):
-                    terms = rotation_terms(
-                        *lookup(table_ref, ids_ref[8 * t : 8 * t + 8, columns])
-                    )
-                    split = (q + 1) * per_octant - 8 * t
-                    if split < 8:
-                        inside = row < split
-                        for n in range(9):
-                            stage_ref[1, u, n] = jnp.where(inside, 0.0, terms[n])
-                        terms = [jnp.where(inside, v, 0.0) for v in terms]
-                    sums = terms if sums is None else [s + v for s, v in zip(sums, terms)]
-                keep_parts(u, octant_entries(sums, per_octant))
+                    words = lookup(table_ref, ids_ref[8 * t : 8 * t + 8, columns], work)
+                    work.appendleft(functools.partial(decode, u, t, words))
+            while work:
+                work.popleft()()
 
             if q < OCTANTS - 1:
                 for u in range(UNROLL):
@@ -687,9 +732,11 @@
                         for action, p in todo[q, late]:
                             action(p)
 
-    total = totals()
+    total = {}
+    totals(total)
     for u in range(UNROLL):
-        spread((steps - 1) * UNROLL + u, u, OCTANTS - 1, total)
+        for part in spread((steps - 1) * UNROLL + u, u, OCTANTS - 1, total):
+            part()
     place(steps - 1)
     finish(OCTANTS - 1)
     rest = sorted(todo[OCTANTS, 0], key=lambda item: ORDER[item[0].__name__] + item[1])
@@ -751,14 +798,8 @@
         stress_out[component] = updated[component]
     owned = [layer_forces(placed, comp, 0) for comp in range(3)]
     for p in range(len(CHUNKS)):
-
-        @pl.loop(1, MEMBERS)
-        def _(i, p=p):
-            hop1(p, i).wait_send()
-
-        @pl.loop(1, GROUPS)
-        def _(i, p=p):
-            hop2(p, i).wait_send()
+        all1(p).wait_send()
+        all2(p).wait_send()
 
     top_copy().wait()
     for comp in range(3):
@@ -826,10 +867,10 @@
             pltpu.VMEM(stress_old.shape, jnp.float32),
             pltpu.SemaphoreType.DMA((5,)),
             pltpu.SemaphoreType.DMA((10,)),
-            pltpu.SemaphoreType.DMA((chunks, MEMBERS)),
-            pltpu.SemaphoreType.DMA((chunks, MEMBERS)),
-            pltpu.SemaphoreType.DMA((chunks, GROUPS)),
-            pltpu.SemaphoreType.DMA((chunks, GROUPS)),
+            pltpu.SemaphoreType.DMA((chunks,)),
+            pltpu.SemaphoreType.DMA((chunks,)),
+            pltpu.SemaphoreType.DMA((chunks,)),
+            pltpu.SemaphoreType.DMA((chunks,)),
             pltpu.SemaphoreType.DMA((4,)),
         ],
         compiler_params=pltpu.CompilerParams(
@@ -851,15 +892,21 @@
     )
 
 
-def handing_kernel(stress_in, forces_in, stress_out, forces_out, sem):
-    copies = [
-        pltpu.make_async_copy(stress_in, stress_out, sem.at[0]),
-        pltpu.make_async_copy(forces_in, forces_out, sem.at[1]),
-    ]
-    for copy in copies:
-        copy.start()
-    for copy in copies:
-        copy.wait()
+def handing_kernel(stress_in, forces_in, stress_out, forces_out, stress_ref, forces_ref, sem):
+    for hop, pairs in enumerate(
+        (
+            ((stress_in, stress_ref), (forces_in, forces_ref)),
+            ((stress_ref, stress_out), (forces_ref, forces_out)),
+        )
+    ):
+        copies = [
+            pltpu.make_async_copy(source, target, sem.at[hop, n])
+            for n, (source, target) in enumerate(pairs)
+        ]
+        for copy in copies:
+            copy.start()
+        for copy in copies:
+            copy.wait()
 
 
 def handed_out(stress, forces):
@@ -869,7 +916,11 @@
         out_shape=tuple(jax.ShapeDtypeStruct(x.shape, x.dtype) for x in (stress, forces)),
         in_specs=[hbm, hbm],
         out_specs=(hbm, hbm),
-        scratch_shapes=[pltpu.SemaphoreType.DMA((2,))],
+        scratch_shapes=[
+            pltpu.VMEM(stress.shape, stress.dtype),
+            pltpu.VMEM(forces.shape, forces.dtype),
+            pltpu.SemaphoreType.DMA((2, 2)),
+        ],
         name="handed_out",
     )(stress, forces)
 

time: 72.6 us -> 68.8 us (0.948)
  Pallas kernels: 71.9 us -> 67.8 us
    pallas_call x1, Pallas kernels: 69.2 us -> 66.4 us  [fused_step(): pl.pallas_call(exchange_kernel, out_shape=(jax.ShapeDtypeStruct(stress_ol...]
    pallas_call x1, Pallas kernels: 2.7 us -> 1.46 us  [handed_out(): pl.pallas_call(handing_kernel, out_shape=tuple((jax.ShapeDtypeStruct(x.sh...]
where the time goes in v5:
time: 68.8 us; the launch traced here: 68.6 us
  Pallas kernels  67.8 us (99%)
  between operations  0.8 us (1%)
    pallas_call x1, Pallas kernels, fused_step(): pl.pallas_call(exchange_kernel, out_shape=(jax.ShapeDtypeStruct(stress_ol...  66.4 us
    pallas_call x1, Pallas kernels, handed_out(): pl.pallas_call(handing_kernel, out_shape=tuple((jax.ShapeDtypeStruct(x.sh...  1.46 us

profile of v5, /device:TPU:1, one launch (start us, length us, event | category | flops | bytes accessed | tf_op | source)
XLA Modules:
  0.0 68.6 jit_solution(8611270475639014195)
XLA Ops:
  0.6 66.4 %fused_step.1 = (f32[6,8,225]{2,1,0:T(8,128)}, f32[3,1,256]{2,1,0:T(1,128)}) custom-call(s32[216,2048]{1,0:T(8,128)} %ids_hbm.1, f32[3,4096]{1,0:T(4,128)} %euler_hbm.1, s32[1,2048]{1,0:T(1,128)} %bitcast.3, s32[1,2048]{1,0:T(1,128)} %bitcast.4, s32[1,2048]{1,0:T(1,128)} %bitcast.5, f32[3,1,256]{2,1,0:T(1,128)} %below_hbm.1, f32[6,8,225]{2,1,0:T(8,128)} %stress_hbm.1, ...), custom_call_target="tpu_custom_call" | custom-call | tf_op jit(solution)/shard_map/fused_step/pallas_call | solution.py:823
  67.0 1.5 %handed_out.1 = (f32[6,8,225]{2,1,0:T(8,128)}, f32[3,1,256]{2,1,0:T(1,128)}) custom-call(f32[6,8,225]{2,1,0:T(8,128)} %get-tuple-element.4.stress_in, f32[3,1,256]{2,1,0:T(1,128)} %get-tuple-element.5.forces_in), custom_call_target="tpu_custom_call" | custom-call | tf_op jit(solution)/shard_map/handed_out/pallas_call | solution.py:914

commit v6 on v5

--- a/solution.py
+++ b/solution.py
@@ -121,11 +121,11 @@
     lanes = ids & 127
     bits = [(ids & (128 << level)) != 0 for level in range(5)]
     words = ([], [])
-    for row in range(32):
-        for n, stack in enumerate(words):
+    for n, stack in enumerate(words):
+        for row in range(32):
             merge_tree(stack, lane_pick(table_ref[n * 32 + row], lanes), row, bits)
-        if work and row % 3 == 2:
-            work.popleft()()
+            if work and row % 5 == 4:
+                work.popleft()()
     return words[0][0], words[1][0]
 
 
@@ -400,6 +400,8 @@
     label_ref,
     part_ref,
     pool_ref,
+    pend_ref,
+    open_ref,
     stage_ref,
     wide_ref,
     acc_ref,
@@ -594,6 +596,8 @@
                     ]
 
     part_ref[...] = jnp.zeros(part_ref.shape, jnp.bfloat16)
+    pend_ref[...] = jnp.zeros(pend_ref.shape, jnp.int32)
+    open_ref[...] = jnp.zeros(open_ref.shape, jnp.float32)
     target = jnp.minimum(lax.broadcasted_iota(jnp.int32, (16, 160), 0), 8)
     source = lax.broadcasted_iota(jnp.int32, (16, 160), 1)
     source = jnp.right_shift(jnp.where(source >= 80, source - 80, source), 3)
@@ -612,6 +616,16 @@
         part_ref[:80, lanes] = high
         part_ref[80:, lanes] = (stacked - high.astype(jnp.float32)).astype(jnp.bfloat16)
 
+    cuts = [min((q + 1) * per_octant - 8 * (-(-(q + 1) * per_octant // 8) - 1), 8) for q in range(OCTANTS)]
+
+    def settle(cut, step):
+        terms = rotation_terms(pend_ref[0], pend_ref[1])
+        inside = row < cut
+        for n in range(9):
+            carry_ref[step * UNROLL + UNROLL - 1, n] = jnp.where(inside, 0.0, terms[n])
+        sums = [open_ref[n] + jnp.where(inside, terms[n], 0.0) for n in range(9)]
+        keep_parts(UNROLL - 1, octant_entries(sums, per_octant))
+
     def totals(out):
         out["sum"] = jnp.dot(pool_ref[...], part_ref[...], preferred_element_type=jnp.float32)
 
@@ -682,7 +696,8 @@
                     stage_ref[0, u] = carry_ref[step * UNROLL + u]
             total = {}
             work = collections.deque()
-            totals(total)
+            work.append(functools.partial(settle, jnp.where(step == 0, cuts[q - 1], cuts[q]), before))
+            work.append(functools.partial(totals, total))
             for u in range(UNROLL):
                 work.extend(spread(before * UNROLL + u, u, label_octant, total))
             work.append(functools.partial(place, before))
@@ -690,9 +705,8 @@
 
             def decode(u, t, words):
                 terms = rotation_terms(*words)
-                split = (q + 1) * per_octant - 8 * t
-                if split < 8:
-                    inside = row < split
+                if t == stop - 1 and cuts[q] < 8:
+                    inside = row < cuts[q]
                     for n in range(9):
                         stage_ref[1, u, n] = jnp.where(inside, 0.0, terms[n])
                     terms = [jnp.where(inside, v, 0.0) for v in terms]
@@ -709,12 +723,16 @@
                 columns = pl.ds(pl.multiple_of((step * UNROLL + u) * 128, 128), 128)
                 for t in range(fresh, stop):
                     words = lookup(table_ref, ids_ref[8 * t : 8 * t + 8, columns], work)
-                    work.appendleft(functools.partial(decode, u, t, words))
+                    if u < UNROLL - 1 or t < stop - 1:
+                        work.appendleft(functools.partial(decode, u, t, words))
             while work:
                 work.popleft()()
-
+            for n in range(2):
+                pend_ref[n] = words[n]
+            for n in range(9):
+                open_ref[n] = state[UNROLL - 1][n]
             if q < OCTANTS - 1:
-                for u in range(UNROLL):
+                for u in range(UNROLL - 1):
                     carry_ref[step * UNROLL + u] = stage_ref[1, u]
 
             @pl.when(step == 0)
@@ -732,6 +750,7 @@
                         for action, p in todo[q, late]:
                             action(p)
 
+    settle(cuts[OCTANTS - 1], steps - 1)
     total = {}
     totals(total)
     for u in range(UNROLL):
@@ -844,6 +863,8 @@
             pltpu.VMEM((blocks, 48, 128), jnp.bfloat16),
             pltpu.VMEM((160, 128 * UNROLL), jnp.bfloat16),
             pltpu.VMEM((16, 160), jnp.bfloat16),
+            pltpu.VMEM((2, 8, 128), jnp.int32),
+            pltpu.VMEM((9, 8, 128), jnp.float32),
             pltpu.VMEM((2, UNROLL, 9, 8, 128), jnp.float32),
             pltpu.VMEM((WORDS, 256 * UNROLL), jnp.bfloat16),
             pltpu.VMEM((DEVICES, WORDS), jnp.float32),

time: 68.8 us -> 68.2 us (level)
  no operation moved by 1% of the time
where the time goes in v6:
time: 68.2 us; the launch traced here: 68 us
  Pallas kernels  67.2 us (99%)
  between operations  0.8 us (1%)
    pallas_call x1, Pallas kernels, fused_step(): pl.pallas_call(exchange_kernel, out_shape=(jax.ShapeDtypeStruct(stress_ol...  65.8 us
    pallas_call x1, Pallas kernels, handed_out(): pl.pallas_call(handing_kernel, out_shape=tuple((jax.ShapeDtypeStruct(x.sh...  1.46 us

profile of v6, /device:TPU:1, one launch (start us, length us, event | category | flops | bytes accessed | tf_op | source)
XLA Modules:
  0.0 68.0 jit_solution(12856555605589133623)
XLA Ops:
  0.6 65.8 %fused_step.1 = (f32[6,8,225]{2,1,0:T(8,128)}, f32[3,1,256]{2,1,0:T(1,128)}) custom-call(s32[216,2048]{1,0:T(8,128)} %ids_hbm.1, f32[3,4096]{1,0:T(4,128)} %euler_hbm.1, s32[1,2048]{1,0:T(1,128)} %bitcast.3, s32[1,2048]{1,0:T(1,128)} %bitcast.4, s32[1,2048]{1,0:T(1,128)} %bitcast.5, f32[3,1,256]{2,1,0:T(1,128)} %below_hbm.1, f32[6,8,225]{2,1,0:T(8,128)} %stress_hbm.1, ...), custom_call_target="tpu_custom_call" | custom-call | tf_op jit(solution)/shard_map/fused_step/pallas_call | solution.py:842
  66.4 1.5 %handed_out.1 = (f32[6,8,225]{2,1,0:T(8,128)}, f32[3,1,256]{2,1,0:T(1,128)}) custom-call(f32[6,8,225]{2,1,0:T(8,128)} %get-tuple-element.4.stress_in, f32[3,1,256]{2,1,0:T(1,128)} %get-tuple-element.5.forces_in), custom_call_target="tpu_custom_call" | custom-call | tf_op jit(solution)/shard_map/handed_out/pallas_call | solution.py:935

commit v7 on v6

--- a/solution.py
+++ b/solution.py
@@ -163,7 +163,7 @@
 NT_DIMS = (((1,), (1,)), ((), ()))
 MESH = pl.DeviceIdType.MESH
 OCTANTS = 8
-CHUNKS = ((0, 2), (2, 4), (4, 5), (5, 6), (6, 7), (7, 8))
+CHUNKS = ((0, 3), (3, 6), (6, 7), (7, 8))
 UNROLL = 4
 WORDS = 384
 ENTRY_ROWS = 8 * CAP
@@ -671,9 +671,9 @@
 
     todo = {}
     for action, times in (
-        (start1, ((2, 0), (4, 0), (5, 0), (6, 0), (7, 0), (8, 0))),
-        (pass_on, ((3, 1), (5, 1), (6, 0), (7, 0), (7, 3), (8, 0))),
-        (take_in, ((4, 3), (6, 3), (7, 3), (8, 0), (8, 0), (8, 0))),
+        (start1, ((3, 0), (6, 0), (7, 0), (8, 0))),
+        (pass_on, ((5, 0), (7, 2), (8, 0), (8, 0))),
+        (take_in, ((6, 3), (8, 0), (8, 0), (8, 0))),
     ):
         for p, time in enumerate(times):
             todo.setdefault(time, []).append((action, p))

time: 68.2 us -> 67.4 us (0.988)
  Pallas kernels: 67.2 us -> 66.4 us
    pallas_call x1, Pallas kernels: 65.8 us -> 65 us  [fused_step(): pl.pallas_call(exchange_kernel, out_shape=(jax.ShapeDtypeStruct(stress_ol...]
where the time goes in v7:
time: 67.4 us; the launch traced here: 67.2 us
  Pallas kernels  66.4 us (99%)
  between operations  0.8 us (1%)
    pallas_call x1, Pallas kernels, fused_step(): pl.pallas_call(exchange_kernel, out_shape=(jax.ShapeDtypeStruct(stress_ol...  65 us
    pallas_call x1, Pallas kernels, handed_out(): pl.pallas_call(handing_kernel, out_shape=tuple((jax.ShapeDtypeStruct(x.sh...  1.46 us

profile of v7, /device:TPU:1, one launch (start us, length us, event | category | flops | bytes accessed | tf_op | source)
XLA Modules:
  0.0 67.2 jit_solution(523156959334914850)
XLA Ops:
  0.6 65.0 %fused_step.1 = (f32[6,8,225]{2,1,0:T(8,128)}, f32[3,1,256]{2,1,0:T(1,128)}) custom-call(s32[216,2048]{1,0:T(8,128)} %ids_hbm.1, f32[3,4096]{1,0:T(4,128)} %euler_hbm.1, s32[1,2048]{1,0:T(1,128)} %bitcast.3, s32[1,2048]{1,0:T(1,128)} %bitcast.4, s32[1,2048]{1,0:T(1,128)} %bitcast.5, f32[3,1,256]{2,1,0:T(1,128)} %below_hbm.1, f32[6,8,225]{2,1,0:T(8,128)} %stress_hbm.1, ...), custom_call_target="tpu_custom_call" | custom-call | tf_op jit(solution)/shard_map/fused_step/pallas_call | solution.py:842
  65.6 1.5 %handed_out.1 = (f32[6,8,225]{2,1,0:T(8,128)}, f32[3,1,256]{2,1,0:T(1,128)}) custom-call(f32[6,8,225]{2,1,0:T(8,128)} %get-tuple-element.4.stress_in, f32[3,1,256]{2,1,0:T(1,128)} %get-tuple-element.5.forces_in), custom_call_target="tpu_custom_call" | custom-call | tf_op jit(solution)/shard_map/handed_out/pallas_call | solution.py:935
